TPU v7x, 256 devices: a whole 4x4x8 slice. The times are simulated.
256 devices in a mesh: seq: 32 (over y, x, core), head: 8 (over z).
Axes of the slice: x: 4, y: 4, z: 8, core: 2. Of those that a mesh axis runs over, the one named last changes fastest.
Arguments:
- queries: bfloat16 [32768, 32, 128], P('seq', 'head'), may hold values from -6 to 6
- keys: bfloat16 [32768, 32, 128], P('seq', 'head'), may hold values from -6 to 6
- values: bfloat16 [32768, 32, 128], P('seq', 'head'), may hold values from -6 to 6
- out_grad: bfloat16 [32768, 32, 128], P('seq', 'head'), may hold values from -6 to 6
- level_codes: int32 [21, 32768], P(None, ('seq', 'head')), may hold values from 1 to 16
Outputs:
- query_grad: bfloat16 [32768, 32, 128], P('seq', 'head')
- key_grad: bfloat16 [32768, 32, 128], P('seq', 'head')
- value_grad: bfloat16 [32768, 32, 128], P('seq', 'head')
Inputs may be any that keep to these rules, and one draw needn't show every extreme that they name: `level_codes`: level codes are whole numbers.
All inputs are finite; a program needn't handle non-finite values.
Results may differ from a plain program's by a relative error of at most 0.0052.
Values sent between devices are 32-bit elements; how exact they have to be, the bound alone decides.
A program may use at most 128 MiB of HBM per device.

v0:
```python
import jax
import jax.numpy as jnp
from jax import lax
from jax.sharding import PartitionSpec as P


def copy_for_each(x, axis):
    copies = jnp.broadcast_to(x, (lax.axis_size(axis), *x.shape))
    return lax.all_to_all(copies, axis, split_axis=0, concat_axis=0, tiled=True)


def in_order(pieces, dim):
    pieces = jnp.moveaxis(pieces, 0, dim)
    shape = pieces.shape
    return pieces.reshape(*shape[:dim], shape[dim] * shape[dim + 1], *shape[dim + 2 :])


def gather_directly(x, axis, dim):
    pieces = copy_for_each(x, axis)
    return in_order(pieces, dim)


def partner(x, axis, apart):
    return lax.ppermute(x, axis, [(i, i ^ 1 << apart) for i in range(lax.axis_size(axis))])


def level_weights(codes):
    order = jnp.arange(codes.shape[0], dtype=jnp.float32)
    factor = jnp.exp2(-0.5 * jnp.maximum(order - 1.0, 0.0)) / 16.0
    return codes.astype(jnp.float32) * factor[:, None]


def level_matrix(count, bits):
    rows = jnp.arange(count, dtype=jnp.int32)[:, None]
    cols = jnp.arange(count, dtype=jnp.int32)[None, :]
    differ = jnp.bitwise_xor(rows, cols)
    depth = jnp.zeros((count, count), jnp.int32)
    for power in range(bits):
        depth = depth + (differ >= 1 << power).astype(jnp.int32)
    return jnp.where(cols <= rows, depth, -1)


def level_mask(depth, lam, bits):
    mask = jnp.zeros(depth.shape, jnp.float32)
    for level in range(bits + 1):
        mask = mask + jnp.where(depth == level, lam[level][:, None], 0.0)
    return mask


def local_head(mask, scale, query, key, value, grad):
    inner = (((1,), (1,)), ((), ()))
    outer = (((0,), (0,)), ((), ()))
    scores = lax.dot_general(query, key, inner, preferred_element_type=jnp.float32)
    dprob = lax.dot_general(grad, value, inner, preferred_element_type=jnp.float32)
    weight_q = (mask * (scale * dprob)).astype(jnp.bfloat16)
    weight_v = (mask * (scale * scores)).astype(jnp.bfloat16)
    dquery = jnp.dot(weight_q, key, preferred_element_type=jnp.float32)
    dkey = lax.dot_general(weight_q, query, outer, preferred_element_type=jnp.float32)
    dvalue = lax.dot_general(weight_v, grad, outer, preferred_element_type=jnp.float32)
    return (dquery, dkey, dvalue)


def on_device(queries, keys, values, out_grad, level_codes):
    count, heads, width = queries.shape
    scale = width ** (-0.5)
    local_bits = count.bit_length() - 1
    tree_bits = lax.axis_size("seq").bit_length() - 1
    here = lax.axis_index("seq")
    codes = gather_directly(level_codes, "head", 1)
    lam = level_weights(codes)
    mask = level_mask(level_matrix(count, local_bits), lam, local_bits)

    def one_head(items):
        query, key, value, grad = items
        return local_head(mask, scale, query, key, value, grad)

    heads_first = (
        jnp.swapaxes(queries, 0, 1),
        jnp.swapaxes(keys, 0, 1),
        jnp.swapaxes(values, 0, 1),
        jnp.swapaxes(out_grad, 0, 1),
    )
    local_q, local_k, local_v = lax.map(one_head, heads_first)
    on_bits = jnp.stack(
        [jnp.bitwise_and(jnp.right_shift(here, b), 1) for b in range(tree_bits)]
    ).astype(jnp.float32)
    lam_cross = lam[local_bits + 1 : local_bits + 1 + tree_bits] * on_bits[:, None]
    state = jnp.einsum("thx,thy->hxy", keys, values, preferred_element_type=jnp.float32)
    query32 = queries.astype(jnp.float32)
    level_list = []
    for b in range(tree_bits):
        weighted = (lam_cross[b][:, None, None] * query32).astype(jnp.bfloat16)
        level_list.append(
            scale
            * jnp.einsum("thx,thy->hxy", weighted, out_grad, preferred_element_type=jnp.float32)
        )
    level_grad = jnp.stack(level_list)
    key_state = jnp.zeros(state.shape, jnp.float32)
    total = state
    found = []
    for b in range(tree_bits):
        other = partner(total, "seq", b)
        summed = total + other
        found.append(summed - total)
        total = summed
    cross = jnp.stack(found)
    pending = level_grad
    for level in range(tree_bits):
        received = partner(pending, "seq", level)
        key_state = key_state + received[0]
        pending = pending[1:] + received[1:]
    cross_half = cross.astype(jnp.bfloat16)
    cross_q = jnp.zeros(queries.shape, jnp.float32)
    for b in range(tree_bits):
        projected = jnp.einsum(
            "thy,hxy->thx", out_grad, cross_half[b], preferred_element_type=jnp.float32
        )
        cross_q = cross_q + lam_cross[b][:, None, None] * projected
    cross_q = scale * cross_q
    key_half = key_state.astype(jnp.bfloat16)
    cross_k = jnp.einsum("hxy,thy->thx", key_half, values, preferred_element_type=jnp.float32)
    cross_v = jnp.einsum("hxy,thx->thy", key_half, keys, preferred_element_type=jnp.float32)
    query_grad = (jnp.swapaxes(local_q, 0, 1) + cross_q).astype(jnp.bfloat16)
    key_grad = (jnp.swapaxes(local_k, 0, 1) + cross_k).astype(jnp.bfloat16)
    value_grad = (jnp.swapaxes(local_v, 0, 1) + cross_v).astype(jnp.bfloat16)
    return (query_grad, key_grad, value_grad)


def solution(mesh):
    return jax.shard_map(
        on_device,
        mesh=mesh,
        in_specs=(
            P("seq", "head", None),
            P("seq", "head", None),
            P("seq", "head", None),
            P("seq", "head", None),
            P(None, ("seq", "head")),
        ),
        out_specs=(P("seq", "head", None), P("seq", "head", None), P("seq", "head", None)),
        check_vma=False,
    )
```

profile of v0, /device:TPU:1, one launch (start us, length us, event | category | flops | bytes accessed | tf_op | source)
XLA Modules:
  0.0 188.1 jit_solution(14224766223599143622)
XLA Ops:
  2.1 9.0 %all-to-all-start = ((s32[8,21,128]{2,1,0:T(8,128)}), s32[8,21,128]{2,1,0:T(8,128)S(1)}, u32[]{:S(2)}, u32[]{:S(2)}) async-start(s32[8,21,128]{2,1,0:T(8,128)} %broadcast_in_dim.116), calls=%async_computation | async-start | bytes 196608 | tf_op jit(solution)/shard_map/all_to_all | solution.py:9
  11.2 7.5 %all-to-all-done = s32[8,21,128]{2,1,0:T(8,128)S(1)} async-done(((s32[8,21,128]{2,1,0:T(8,128)}), s32[8,21,128]{2,1,0:T(8,128)S(1)}, u32[]{:S(2)}, u32[]{:S(2)}) %all-to-all-start) | async-done | bytes 86048 | tf_op jit(solution)/shard_map/all_to_all | solution.py:9
  19.0 6.6 %fusion.63 = (bf16[1024,4,128]{2,1,0:T(4,128)(2,1)S(1)}, bf16[1024,4,128]{2,1,0:T(4,128)(2,1)S(1)}, bf16[1024,4,128]{2,1,0:T(4,128)(2,1)S(1)}, bf16[1024,4,128]{2,1,0:T(4,128)(2,1)S(1)}, bf16[1024,4,128]{2,1,0:T(4,128)(2,1)S(1)}) fusion(bf16[1024,4,128]{2,1,0:T(4,128)(2,1)S(1)} %copy-done.2, f32[1024]{0:T(1024)S(1)} %bitcast.137, f32[1024]{0:T(1024)S(1)} %bitcast.143, ...), kind=kLoop, calls=%fused_computation.70 | loop fusion | flops 5767168 | bytes 6311936 | tf_op jit(solution)/shard_map/convert_element_type | solution.py:92
  28.8 2.1 %collective-permute-start.5 = (f32[5,4,128,128]{3,2,1,0:T(8,128)S(1)}, f32[5,4,128,128]{3,2,1,0:T(8,128)S(1)}, u32[]{:S(2)}, u32[]{:S(2)}) collective-permute-start(f32[5,4,128,128]{3,2,1,0:T(8,128)S(1)} %get-tuple-element.180), channel_id=1, source_target_pairs={{0,8},{8,0},{16,24},{24,16},{32,40},{40,32},{48,56},{56,48},{64,72... | collective-permute-start | bytes 3932168 | tf_op jit(solution)/shard_map/ppermute | solution.py:24
  31.0 2.7 %collective-permute-done.5 = f32[5,4,128,128]{3,2,1,0:T(8,128)S(1)} collective-permute-done((f32[5,4,128,128]{3,2,1,0:T(8,128)S(1)}, f32[5,4,128,128]{3,2,1,0:T(8,128)S(1)}, u32[]{:S(2)}, u32[]{:S(2)}) %collective-permute-start.5) | collective-permute-done | bytes 1310752 | tf_op jit(solution)/shard_map/ppermute | solution.py:24
  42.1 18.2 %collective-permute-done.6 = f32[4,4,128,128]{3,2,1,0:T(8,128)S(1)} collective-permute-done((f32[4,4,128,128]{3,2,1,0:T(8,128)}, f32[4,4,128,128]{3,2,1,0:T(8,128)S(1)}, u32[]{:S(2)}, u32[]{:S(2)}) %collective-permute-start.6) | collective-permute-done | bytes 1048608 | tf_op jit(solution)/shard_map/ppermute | solution.py:24
  60.4 2.5 %slice_add_fusion.1 = f32[3,4,128,128]{3,2,1,0:T(8,128)} fusion(f32[4,4,128,128]{3,2,1,0:T(8,128)S(1)} %collective-permute-done.6, f32[4,4,128,128]{3,2,1,0:T(8,128)} %slice_add_fusion), kind=kLoop, calls=%fused_computation.102 | loop fusion | flops 196608 | bytes 2359296 | tf_op jit(solution)/shard_map/add | solution.py:111
  62.9 2.7 %collective-permute-start.7 = (f32[3,4,128,128]{3,2,1,0:T(8,128)}, f32[3,4,128,128]{3,2,1,0:T(8,128)}, u32[]{:S(2)}, u32[]{:S(2)}) collective-permute-start(f32[3,4,128,128]{3,2,1,0:T(8,128)} %slice_add_fusion.1), channel_id=1, source_target_pairs={{0,32},{8,40},{16,48},{24,56},{32,0},{40,8},{48,16},{56,24},{64,96... | collective-permute-start | bytes 2359304 | tf_op jit(solution)/shard_map/ppermute | solution.py:24
  65.6 70.5 %while.15 = (s32[]{:T(128)}, f32[4,1024,128]{1,2,0:T(8,128)}, f32[4,1024,128]{1,2,0:T(8,128)}, f32[4,1024,128]{1,2,0:T(8,128)}, bf16[4,1024,128]{2,1,0:T(8,128)(...) while((s32[]{:T(128)}, f32[4,1024,128]{1,2,0:T(8,128)}, ...), condition=%wide.region_1.2_spmd.clone, body=%wide.region_0.1_spmd.clone.sunk | while | flops 1482686464 | bytes 9794749 | solution.py:83
  65.6 10.9 %multiply_convert_fusion.3 = bf16[1024,1024]{1,0:T(8,128)(2,1)S(1)} fusion(f32[1024]{0:T(1024)S(1)} %get-tuple-element.357, f32[1024]{0:T(1024)S(1)} %get-tuple-element.356, f32[1024]{0:T(1024)S(1)} %get-tuple-element.355, f32[1024]{0:T(1024)S(1)} %get-tuple-element.354, f32[1024]{0:T(1024)S(1)} %get-tuple-element.353, ...), kind=kOutput, calls=%fused_computation.16.clone.1 | convolution fusion | flops 338690048 | bytes 2667520 | tf_op jit(solution)/shard_map/while/body/eval_jaxpr/dot_general | solution.py:54
  79.5 3.8 %fusion.131 = f32[4,1024,128]{1,2,0:T(8,128)} fusion(f32[4,1024,128]{1,2,0:T(8,128)} %get-tuple-element.322, s32[]{:T(128)S(6)} %copy.174, f32[1024]{0:T(1024)S(1)} %get-tuple-element.357, f32[1024]{0:T(1024)S(1)} %get-tuple-element.356, f32[1024]{0:T(1024)S(1)} %get-tuple-element.355, f32[1024]{0:T(1024)S(1)} %get-tuple-element.354, ...), kind=kOutput, calls=%fused_computation.23.clone.1 | convolution fusion | flops 607125504 | bytes 1357824 | tf_op jit(solution)/shard_map/while/body/eval_jaxpr/dot_general | solution.py:59
  83.3 10.8 %multiply_convert_fusion.3 = bf16[1024,1024]{1,0:T(8,128)(2,1)S(1)} fusion(f32[1024]{0:T(1024)S(1)} %get-tuple-element.357, f32[1024]{0:T(1024)S(1)} %get-tuple-element.356, f32[1024]{0:T(1024)S(1)} %get-tuple-element.355, f32[1024]{0:T(1024)S(1)} %get-tuple-element.354, f32[1024]{0:T(1024)S(1)} %get-tuple-element.353, ...), kind=kOutput, calls=%fused_computation.16.clone.1 | convolution fusion | flops 338690048 | bytes 2667520 | tf_op jit(solution)/shard_map/while/body/eval_jaxpr/dot_general | solution.py:54
  97.1 3.9 %fusion.131 = f32[4,1024,128]{1,2,0:T(8,128)} fusion(f32[4,1024,128]{1,2,0:T(8,128)} %get-tuple-element.322, s32[]{:T(128)S(6)} %copy.174, f32[1024]{0:T(1024)S(1)} %get-tuple-element.357, f32[1024]{0:T(1024)S(1)} %get-tuple-element.356, f32[1024]{0:T(1024)S(1)} %get-tuple-element.355, f32[1024]{0:T(1024)S(1)} %get-tuple-element.354, ...), kind=kOutput, calls=%fused_computation.23.clone.1 | convolution fusion | flops 607125504 | bytes 1357824 | tf_op jit(solution)/shard_map/while/body/eval_jaxpr/dot_general | solution.py:59
  100.9 10.8 %multiply_convert_fusion.3 = bf16[1024,1024]{1,0:T(8,128)(2,1)S(1)} fusion(f32[1024]{0:T(1024)S(1)} %get-tuple-element.357, f32[1024]{0:T(1024)S(1)} %get-tuple-element.356, f32[1024]{0:T(1024)S(1)} %get-tuple-element.355, f32[1024]{0:T(1024)S(1)} %get-tuple-element.354, f32[1024]{0:T(1024)S(1)} %get-tuple-element.353, ...), kind=kOutput, calls=%fused_computation.16.clone.1 | convolution fusion | flops 338690048 | bytes 2667520 | tf_op jit(solution)/shard_map/while/body/eval_jaxpr/dot_general | solution.py:54
  114.7 3.8 %fusion.131 = f32[4,1024,128]{1,2,0:T(8,128)} fusion(f32[4,1024,128]{1,2,0:T(8,128)} %get-tuple-element.322, s32[]{:T(128)S(6)} %copy.174, f32[1024]{0:T(1024)S(1)} %get-tuple-element.357, f32[1024]{0:T(1024)S(1)} %get-tuple-element.356, f32[1024]{0:T(1024)S(1)} %get-tuple-element.355, f32[1024]{0:T(1024)S(1)} %get-tuple-element.354, ...), kind=kOutput, calls=%fused_computation.23.clone.1 | convolution fusion | flops 607125504 | bytes 1357824 | tf_op jit(solution)/shard_map/while/body/eval_jaxpr/dot_general | solution.py:59
  118.5 10.8 %multiply_convert_fusion.3 = bf16[1024,1024]{1,0:T(8,128)(2,1)S(1)} fusion(f32[1024]{0:T(1024)S(1)} %get-tuple-element.357, f32[1024]{0:T(1024)S(1)} %get-tuple-element.356, f32[1024]{0:T(1024)S(1)} %get-tuple-element.355, f32[1024]{0:T(1024)S(1)} %get-tuple-element.354, f32[1024]{0:T(1024)S(1)} %get-tuple-element.353, ...), kind=kOutput, calls=%fused_computation.16.clone.1 | convolution fusion | flops 338690048 | bytes 2667520 | tf_op jit(solution)/shard_map/while/body/eval_jaxpr/dot_general | solution.py:54
  132.2 3.8 %fusion.131 = f32[4,1024,128]{1,2,0:T(8,128)} fusion(f32[4,1024,128]{1,2,0:T(8,128)} %get-tuple-element.322, s32[]{:T(128)S(6)} %copy.174, f32[1024]{0:T(1024)S(1)} %get-tuple-element.357, f32[1024]{0:T(1024)S(1)} %get-tuple-element.356, f32[1024]{0:T(1024)S(1)} %get-tuple-element.355, f32[1024]{0:T(1024)S(1)} %get-tuple-element.354, ...), kind=kOutput, calls=%fused_computation.23.clone.1 | convolution fusion | flops 607125504 | bytes 1357824 | tf_op jit(solution)/shard_map/while/body/eval_jaxpr/dot_general | solution.py:59
  139.0 4.6 %collective-permute-done.1 = f32[4,128,128]{2,1,0:T(8,128)S(1)} collective-permute-done((f32[4,128,128]{2,1,0:T(8,128)S(1)}, f32[4,128,128]{2,1,0:T(8,128)S(1)}, u32[]{:S(2)}, u32[]{:S(2)}) %collective-permute-start.1) | collective-permute-done | bytes 262176 | tf_op jit(solution)/shard_map/ppermute | solution.py:24
  145.0 5.4 %collective-permute-done.2 = f32[4,128,128]{2,1,0:T(8,128)S(1)} collective-permute-done((f32[4,128,128]{2,1,0:T(8,128)S(1)}, f32[4,128,128]{2,1,0:T(8,128)S(1)}, u32[]{:S(2)}, u32[]{:S(2)}) %collective-permute-start.2) | collective-permute-done | bytes 262176 | tf_op jit(solution)/shard_map/ppermute | solution.py:24
  155.9 3.0 %collective-permute-start.4 = (f32[4,128,128]{2,1,0:T(8,128)S(1)}, f32[4,128,128]{2,1,0:T(8,128)S(1)}, u32[]{:S(2)}, u32[]{:S(2)}) collective-permute-start(f32[4,128,128]{2,1,0:T(8,128)S(1)} %add.340), channel_id=1, source_target_pairs={{0,128},{8,136},{16,144},{24,152},{32,160},{40,168},{48,176},{56,1... | collective-permute-start | bytes 786440 | tf_op jit(solution)/shard_map/ppermute | solution.py:24
  159.3 6.8 %collective-permute-done.8 = f32[2,4,128,128]{3,2,1,0:T(8,128)S(1)} collective-permute-done((f32[2,4,128,128]{3,2,1,0:T(8,128)S(1)}, f32[2,4,128,128]{3,2,1,0:T(8,128)S(1)}, u32[]{:S(2)}, u32[]{:S(2)}) %collective-permute-start.8) | collective-permute-done | bytes 524320 | tf_op jit(solution)/shard_map/ppermute | solution.py:24
  166.2 3.2 %collective-permute-start.9 = (f32[1,4,128,128]{3,2,1,0:T(8,128)S(1)}, f32[1,4,128,128]{3,2,1,0:T(8,128)}, u32[]{:S(2)}, u32[]{:S(2)}) collective-permute-start(f32[1,4,128,128]{3,2,1,0:T(8,128)S(1)} %slice_add_fusion.3), channel_id=1, source_target_pairs={{0,128},{8,136},{16,144},{24,152},{32,160},{40,168},{48,176},{56,1... | collective-permute-start | bytes 786440 | tf_op jit(solution)/shard_map/ppermute | solution.py:24
  169.4 4.5 %collective-permute-done.4 = f32[4,128,128]{2,1,0:T(8,128)S(1)} collective-permute-done((f32[4,128,128]{2,1,0:T(8,128)S(1)}, f32[4,128,128]{2,1,0:T(8,128)S(1)}, u32[]{:S(2)}, u32[]{:S(2)}) %collective-permute-start.4) | collective-permute-done | bytes 262176 | tf_op jit(solution)/shard_map/ppermute | solution.py:24
  176.5 3.3 %collective-permute-done.9 = f32[1,4,128,128]{3,2,1,0:T(8,128)} collective-permute-done((f32[1,4,128,128]{3,2,1,0:T(8,128)S(1)}, f32[1,4,128,128]{3,2,1,0:T(8,128)}, u32[]{:S(2)}, u32[]{:S(2)}) %collective-permute-start.9) | collective-permute-done | bytes 262176 | tf_op jit(solution)/shard_map/ppermute | solution.py:24
  (107 shorter events, 46.0 us)
Async XLA Ops:
  0.6 18.4 %copy-start.2 = (bf16[1024,4,128]{2,1,0:T(4,128)(2,1)S(1)}, bf16[1024,4,128]{2,1,0:T(4,128)(2,1)}, u32[]{:S(2)}) copy-start(bf16[1024,4,128]{2,1,0:T(4,128)(2,1)} %param.7) | copy-start | bytes 3145732
  2.1 16.6 %all-to-all-start = ((s32[8,21,128]{2,1,0:T(8,128)}), s32[8,21,128]{2,1,0:T(8,128)S(1)}, u32[]{:S(2)}, u32[]{:S(2)}) async-start(s32[8,21,128]{2,1,0:T(8,128)} %broadcast_in_dim.116), calls=%async_computation | async-start | bytes 196608 | tf_op jit(solution)/shard_map/all_to_all | solution.py:9
  19.0 6.7 %copy-start.14 = (f32[1,1024]{1,0:T(1,128)}, f32[1,1024]{1,0:T(1,128)S(1)}, u32[]{:S(2)}) copy-start(f32[1,1024]{1,0:T(1,128)S(1)} %get-tuple-element.169) | copy-start | bytes 12292
  19.0 6.7 %copy-start.16 = (f32[1,1024]{1,0:T(1,128)}, f32[1,1024]{1,0:T(1,128)S(1)}, u32[]{:S(2)}) copy-start(f32[1,1024]{1,0:T(1,128)S(1)} %get-tuple-element.170) | copy-start | bytes 12292
  28.8 8.2 %copy-start.3 = (bf16[1024,4,128]{2,1,0:T(4,128)(2,1)S(1)}, bf16[1024,4,128]{2,1,0:T(4,128)(2,1)}, u32[]{:S(2)}) copy-start(bf16[1024,4,128]{2,1,0:T(4,128)(2,1)} %param.9) | copy-start | bytes 3145732
  28.8 8.2 %copy-start.6 = (bf16[1024,4,128]{2,1,0:T(4,128)(2,1)S(1)}, bf16[1024,4,128]{2,1,0:T(4,128)(2,1)}, u32[]{:S(2)}) copy-start(bf16[1024,4,128]{2,1,0:T(4,128)(2,1)} %param.8) | copy-start | bytes 3145732
  28.8 4.8 %collective-permute-start.5 = (f32[5,4,128,128]{3,2,1,0:T(8,128)S(1)}, f32[5,4,128,128]{3,2,1,0:T(8,128)S(1)}, u32[]{:S(2)}, u32[]{:S(2)}) collective-permute-start(f32[5,4,128,128]{3,2,1,0:T(8,128)S(1)} %get-tuple-element.180), channel_id=1, source_target_pairs={{0,8},{8,0},{16,24},{24,16},{32,40},{40,32},{48,56},{56,48},{64,72... | collective-permute-start | bytes 3932168 | tf_op jit(solution)/shard_map/ppermute | solution.py:24
  35.8 24.6 %collective-permute-start.6 = (f32[4,4,128,128]{3,2,1,0:T(8,128)}, f32[4,4,128,128]{3,2,1,0:T(8,128)S(1)}, u32[]{:S(2)}, u32[]{:S(2)}) collective-permute-start(f32[4,4,128,128]{3,2,1,0:T(8,128)} %slice_add_fusion), channel_id=1, source_target_pairs={{0,16},{8,24},{16,0},{24,8},{32,48},{40,56},{48,32},{56,40},{64,80... | collective-permute-start | bytes 3145736 | tf_op jit(solution)/shard_map/ppermute | solution.py:24
  38.3 97.8 %collective-permute-start = (f32[4,128,128]{2,1,0:T(8,128)}, f32[4,128,128]{2,1,0:T(8,128)}, u32[]{:S(2)}, u32[]{:S(2)}) collective-permute-start(f32[4,128,128]{2,1,0:T(8,128)} %fusion.78), channel_id=1, source_target_pairs={{0,8},{8,0},{16,24},{24,16},{32,40},{40,32},{48,56},{56,48},{64,72... | collective-permute-start | bytes 786440 | tf_op jit(solution)/shard_map/ppermute | solution.py:24
  62.9 89.0 %collective-permute-start.7 = (f32[3,4,128,128]{3,2,1,0:T(8,128)}, f32[3,4,128,128]{3,2,1,0:T(8,128)}, u32[]{:S(2)}, u32[]{:S(2)}) collective-permute-start(f32[3,4,128,128]{3,2,1,0:T(8,128)} %slice_add_fusion.1), channel_id=1, source_target_pairs={{0,32},{8,40},{16,48},{24,56},{32,0},{40,8},{48,16},{56,24},{64,96... | collective-permute-start | bytes 2359304 | tf_op jit(solution)/shard_map/ppermute | solution.py:24
  65.6 72.0 %copy-start.1 = (bf16[1024,4,128]{2,1,0:T(4,128)(2,1)S(1)}, bf16[1024,4,128]{2,1,0:T(4,128)(2,1)}, u32[]{:S(2)}) copy-start(bf16[1024,4,128]{2,1,0:T(4,128)(2,1)} %param.10) | copy-start | bytes 3145732
  137.1 6.4 %collective-permute-start.1 = (f32[4,128,128]{2,1,0:T(8,128)S(1)}, f32[4,128,128]{2,1,0:T(8,128)S(1)}, u32[]{:S(2)}, u32[]{:S(2)}) collective-permute-start(f32[4,128,128]{2,1,0:T(8,128)S(1)} %add.335), channel_id=1, source_target_pairs={{0,16},{8,24},{16,0},{24,8},{32,48},{40,56},{48,32},{56,40},{64,80... | collective-permute-start | bytes 786440 | tf_op jit(solution)/shard_map/ppermute | solution.py:24
  143.6 6.8 %collective-permute-start.2 = (f32[4,128,128]{2,1,0:T(8,128)S(1)}, f32[4,128,128]{2,1,0:T(8,128)S(1)}, u32[]{:S(2)}, u32[]{:S(2)}) collective-permute-start(f32[4,128,128]{2,1,0:T(8,128)S(1)} %add.336), channel_id=1, source_target_pairs={{0,32},{8,40},{16,48},{24,56},{32,0},{40,8},{48,16},{56,24},{64,96... | collective-permute-start | bytes 786440 | tf_op jit(solution)/shard_map/ppermute | solution.py:24
  150.5 5.3 %collective-permute-start.3 = (f32[4,128,128]{2,1,0:T(8,128)S(1)}, f32[4,128,128]{2,1,0:T(8,128)S(1)}, u32[]{:S(2)}, u32[]{:S(2)}) collective-permute-start(f32[4,128,128]{2,1,0:T(8,128)S(1)} %add.338), channel_id=1, source_target_pairs={{0,64},{8,72},{16,80},{24,88},{32,96},{40,104},{48,112},{56,120},{... | collective-permute-start | bytes 786440 | tf_op jit(solution)/shard_map/ppermute | solution.py:24
  153.1 13.0 %collective-permute-start.8 = (f32[2,4,128,128]{3,2,1,0:T(8,128)S(1)}, f32[2,4,128,128]{3,2,1,0:T(8,128)S(1)}, u32[]{:S(2)}, u32[]{:S(2)}) collective-permute-start(f32[2,4,128,128]{3,2,1,0:T(8,128)S(1)} %slice_add_fusion.2), channel_id=1, source_target_pairs={{0,64},{8,72},{16,80},{24,88},{32,96},{40,104},{48,112},{56,120},{... | collective-permute-start | bytes 1572872 | tf_op jit(solution)/shard_map/ppermute | solution.py:24
  155.8 18.1 %copy-start.9 = (f32[4,1024,128]{1,2,0:T(8,128)S(1)}, f32[4,1024,128]{1,2,0:T(8,128)}, u32[]{:S(2)}) copy-start(f32[4,1024,128]{1,2,0:T(8,128)} %get-tuple-element.52) | copy-start | bytes 6291460
  155.8 18.1 %copy-start.15 = (f32[1,1024]{1,0:T(1,128)S(1)}, f32[1,1024]{1,0:T(1,128)}, u32[]{:S(2)}) copy-start(f32[1,1024]{1,0:T(1,128)} %copy-done.14) | copy-start | bytes 12292
  155.8 18.1 %copy-start.17 = (f32[1,1024]{1,0:T(1,128)S(1)}, f32[1,1024]{1,0:T(1,128)}, u32[]{:S(2)}) copy-start(f32[1,1024]{1,0:T(1,128)} %copy-done.16) | copy-start | bytes 12292
  155.8 18.1 %copy-start.19 = (f32[1,1024]{1,0:T(1,128)S(1)}, f32[1,1024]{1,0:T(1,128)}, u32[]{:S(2)}) copy-start(f32[1,1024]{1,0:T(1,128)} %copy-done.18) | copy-start | bytes 12292
  155.9 18.1 %copy-start.21 = (f32[1,1024]{1,0:T(1,128)S(1)}, f32[1,1024]{1,0:T(1,128)}, u32[]{:S(2)}) copy-start(f32[1,1024]{1,0:T(1,128)} %copy-done.20) | copy-start | bytes 12292
  155.9 18.1 %copy-start.23 = (f32[1,1024]{1,0:T(1,128)S(1)}, f32[1,1024]{1,0:T(1,128)}, u32[]{:S(2)}) copy-start(f32[1,1024]{1,0:T(1,128)} %copy-done.22) | copy-start | bytes 12292
  155.9 18.0 %collective-permute-start.4 = (f32[4,128,128]{2,1,0:T(8,128)S(1)}, f32[4,128,128]{2,1,0:T(8,128)S(1)}, u32[]{:S(2)}, u32[]{:S(2)}) collective-permute-start(f32[4,128,128]{2,1,0:T(8,128)S(1)} %add.340), channel_id=1, source_target_pairs={{0,128},{8,136},{16,144},{24,152},{32,160},{40,168},{48,176},{56,1... | collective-permute-start | bytes 786440 | tf_op jit(solution)/shard_map/ppermute | solution.py:24
  166.1 7.8 %copy-start.12 = (f32[2,4,128,128]{3,2,1,0:T(8,128)}, f32[2,4,128,128]{3,2,1,0:T(8,128)S(1)}, u32[]{:S(2)}) copy-start(f32[2,4,128,128]{3,2,1,0:T(8,128)S(1)} %collective-permute-done.8) | copy-start | bytes 1572868
  166.2 13.7 %collective-permute-start.9 = (f32[1,4,128,128]{3,2,1,0:T(8,128)S(1)}, f32[1,4,128,128]{3,2,1,0:T(8,128)}, u32[]{:S(2)}, u32[]{:S(2)}) collective-permute-start(f32[1,4,128,128]{3,2,1,0:T(8,128)S(1)} %slice_add_fusion.3), channel_id=1, source_target_pairs={{0,128},{8,136},{16,144},{24,152},{32,160},{40,168},{48,176},{56,1... | collective-permute-start | bytes 786440 | tf_op jit(solution)/shard_map/ppermute | solution.py:24
  (11 other events, 48.9 us)
where the time goes:
time: 191 us; the launch traced here: 188 us
  matrix products  82.7 us (43%)
  waiting for transfers between devices  55.1 us (29%)
  starting transfers between devices  24.9 us (13%)
  other arithmetic  14.1 us (7%)
  local copies, waits for them, and re-layouts  10.3 us (5%)
    ppermute x10, waiting for transfers between devices, partner(): lax.ppermute(x, axis, [(i, i ^ 1 << apart) for i in range(lax.axis_size(a...  47.6 us
    dot_general x4, matrix products, local_head(): lax.dot_general(grad, value, inner, preferred_element_type=jnp.float32)  43.3 us
    ppermute x10, starting transfers between devices, partner(): lax.ppermute(x, axis, [(i, i ^ 1 << apart) for i in range(lax.axis_size(a...  15.9 us
    dot_general x4, matrix products, local_head(): lax.dot_general(weight_v, grad, outer, preferred_element_type=jnp.float32)  15.3 us
    all_to_all x1, starting transfers between devices, copy_for_each(): return lax.all_to_all(copies, axis, split_axis=0, concat_axis=0, tiled=True)  9 us
    all_to_all x1, waiting for transfers between devices, copy_for_each(): return lax.all_to_all(copies, axis, split_axis=0, concat_axis=0, tiled=True)  7.51 us
    unnamed x55, local copies, waits for them, and re-layouts  7.44 us
    convert_element_type x1, other arithmetic, on_device(): weighted = (lam_cross[b][:, None, None] * query32).astype(jnp.bfloat16)  6.62 us
  transfers between devices with their start and end apart: 11, of which 9 were waited for; matrix products, arithmetic and copies ran while one was open for 45% of the time, Pallas kernels for 0%

commit v1 on v0

v1 whole, which is shorter than its diff:
```python
import functools

import jax
import jax.numpy as jnp
from jax import lax
from jax.experimental import pallas as pl
from jax.experimental.pallas import tpu as pltpu
from jax.sharding import PartitionSpec as P

MESH = pl.DeviceIdType.MESH
F32 = jnp.float32
BF16 = jnp.bfloat16
CHUNK = 128
INNER = 3
CROSS = 5
ROWS = 16
PARTNERS = (1, 2, 6, 8, 24)

NN = (((1,), (0,)), ((), ()))
NT = (((1,), (1,)), ((), ()))
TN = (((0,), (0,)), ((), ()))


def dot(a, b, dims=NN):
    return lax.dot_general(a, b, dims, preferred_element_type=F32)


def factor(level):
    return 2.0 ** (-0.5 * max(level - 1, 0)) / 16.0


def on_bit(index, bit):
    return lax.rem(jnp.right_shift(index, bit), 2).astype(F32)


def spread(codes, first, count):
    rows = lax.broadcasted_iota(jnp.int32, (codes.shape[0], count * CHUNK), 0)
    cols = lax.broadcasted_iota(jnp.int32, (codes.shape[0], count * CHUNK), 1)
    pick = (rows == first + jnp.right_shift(cols, 7)).astype(F32).astype(BF16)
    return dot(codes.astype(F32).astype(BF16), pick, TN)


def split_heads(flat, tmp, out):
    heads, count, _ = out.shape
    tmp[...] = flat[...].astype(F32)
    for h in range(heads):
        out[h] = tmp[pl.ds(h, count, stride=heads), :].astype(BF16)


def exchange_kernel(
    scale, zs,
    q_in, k_in, v_in, g_in, codes_in,
    qh_out, kh_out, vh_out, gh_out, codes_out, cross_out, ks_out,
    flat, tmp, qh, kh, vh, gh, lam, weighted,
    state, r_state, tot, r_tot, r_found,
    level, r_level, r_level0, down, r_down, mid, r_mid,
    in_sem, out_sem, code_send, code_recv, send, recv,
):
    seq = lax.axis_index("seq")
    z = lax.axis_index("head")
    mine = 2 * lax.rem(seq, 2)
    theirs = 2 - mine
    heads, count, _ = qh.shape
    partner = [jnp.bitwise_xor(seq, p) for p in PARTNERS]

    barrier = pltpu.get_barrier_semaphore()
    for p in partner:
        pl.semaphore_signal(barrier, inc=1, device_id=(p, z), device_id_type=MESH)
    for d in range(1, zs):
        pl.semaphore_signal(
            barrier, inc=1, device_id=(seq, lax.rem(z + d, zs)), device_id_type=MESH)

    loads = [
        pltpu.make_async_copy(src, flat.at[i], in_sem.at[i])
        for i, src in enumerate((k_in, v_in, q_in, g_in))
    ]
    for c in loads:
        c.start()

    sent = []

    def remote(src, dst, to):
        n = len(sent)
        c = pltpu.make_async_remote_copy(
            src_ref=src, dst_ref=dst, send_sem=send.at[n], recv_sem=recv.at[n],
            device_id=(partner[to], z), device_id_type=MESH)
        sent.append(c)
        c.start()
        return c

    outs = []

    def put(i, src, dst):
        c = pltpu.make_async_copy(src, dst, out_sem.at[i])
        c.start()
        outs.append(c)

    loads[0].wait()
    split_heads(flat.at[0], tmp, kh)
    put(0, kh, kh_out)
    loads[1].wait()
    split_heads(flat.at[1], tmp, vh)
    put(1, vh, vh_out)
    for h in range(heads):
        state[h] = dot(vh[h], kh[h], TN)

    pl.semaphore_wait(barrier, len(partner) + zs - 1)
    codes_sent = []
    for d in range(1, zs):
        c = pltpu.make_async_remote_copy(
            src_ref=codes_in, dst_ref=codes_out.at[z], send_sem=code_send.at[d - 1],
            recv_sem=code_recv.at[d - 1], device_id=(seq, lax.rem(z + d, zs)),
            device_id_type=MESH)
        c.start()
        codes_sent.append(c)
    s_their = remote(state.at[pl.ds(theirs, 2)], r_state.at[pl.ds(theirs, 2)], 0)
    s_mine = remote(state.at[pl.ds(mine, 2)], r_state.at[pl.ds(mine, 2)], 0)
    codes_out[z] = codes_in[...]

    loads[2].wait()
    split_heads(flat.at[2], tmp, qh)
    put(2, qh, qh_out)

    s_their.wait_recv()
    up = []
    now = []
    for i in range(2):
        tot[0, i] = state[mine + i] + r_state[mine + i]
        now.append(remote(tot.at[0, i], r_tot.at[0, i], 1))
    up.append(now)

    loads[3].wait()
    split_heads(flat.at[3], tmp, gh)
    put(3, gh, gh_out)

    def step_up(p):
        now = []
        for i in range(2):
            up[p - 1][i].wait_recv()
            tot[p, i] = tot[p - 1, i] + r_tot[p - 1, i]
            now.append(remote(tot.at[p, i], r_tot.at[p, i], p + 1))
        up.append(now)

    for c in codes_sent:
        c.wait_recv()

    @pl.loop(0, zs)
    def _(c):
        wide = spread(codes_out[c], 11, CROSS)
        for b in range(CROSS):
            cols = pl.ds(b * CHUNK, CHUNK)
            lam[pl.ds(c * CHUNK, CHUNK), cols] = wide[:, b * CHUNK : (b + 1) * CHUNK] * (
                factor(11 + b) * on_bit(seq, b))

    step_up(1)

    @pl.loop(0, heads)
    def _(h):
        query = qh[h].astype(F32)
        for b in range(CROSS):
            cols = pl.ds(b * CHUNK, CHUNK)
            weighted[:, cols] = (lam[:, cols] * query).astype(BF16)
        result = dot(gh[h], weighted[...], TN)
        for b in range(CROSS):
            level[b, h] = scale * result[:, b * CHUNK : (b + 1) * CHUNK]

    halves = [None] * CROSS
    for b in (4, 3, 2, 1):
        halves[b] = remote(
            level.at[b, pl.ds(theirs, 2)], r_level.at[b - 1, pl.ds(theirs, 2)], 0)
    whole = remote(level.at[0], r_level0, 0)

    step_up(2)
    halves[4].wait_recv()
    down_now = []
    for i in range(2):
        down[0, i] = level[4, mine + i] + r_level[3, mine + i]
        down_now.append(remote(down.at[0, i], r_down.at[0, i], 4))
    step_up(3)
    for n, b in enumerate((3, 2, 1)):
        halves[b].wait_recv()
        after = []
        for i in range(2):
            down_now[i].wait_recv()
            if n == 0:
                mid[n, i] = r_down[n, i]
            else:
                mid[n, i] = mid[n - 1, i] + r_down[n, i]
            down[n + 1, i] = mid[n, i] + level[b, mine + i] + r_level[b - 1, mine + i]
            after.append(remote(down.at[n + 1, i], r_down.at[n + 1, i], b))
        down_now = after
        if n == 1:
            found = []
            for p in range(4):
                for i in range(2):
                    if p == 3:
                        up[p][i].wait_recv()
                    found.append(remote(r_tot.at[p, i], r_found.at[p, i], 0))
    last = []
    for i in range(2):
        down_now[i].wait_recv()
        mid[3, i] = mid[2, i] + r_down[3, i]
        last.append(remote(mid.at[3, i], r_mid.at[i], 0))

    s_mine.wait_recv()
    for h in range(heads):
        cross_out[0, h] = r_state[h].astype(BF16)
    for p in range(4):
        for i in range(2):
            found[2 * p + i].wait_recv()
            cross_out[p + 1, mine + i] = r_tot[p, i].astype(BF16)
            cross_out[p + 1, theirs + i] = r_found[p, i].astype(BF16)
    whole.wait_recv()
    for i in range(2):
        ks_out[mine + i] = mid[3, i] + r_level0[mine + i]
    for i in range(2):
        last[i].wait_recv()
        ks_out[theirs + i] = r_mid[i] + r_level0[theirs + i]

    for c in sent + codes_sent:
        c.wait_send()
    for c in outs:
        c.wait()


def exchange(scale, zs, q, k, v, g, codes):
    heads, count, width = 4, q.shape[0] // 4, q.shape[1]
    square = (width, width)
    any_space = pl.BlockSpec(memory_space=pl.ANY)
    vmem = pl.BlockSpec(memory_space=pltpu.VMEM)
    split = jax.ShapeDtypeStruct((heads, count, width), BF16)
    messages = 2 + 8 + 8 + 4 + 1 + 8 + 2
    return pl.pallas_call(
        functools.partial(exchange_kernel, scale, zs),
        out_shape=(
            split, split, split, split,
            jax.ShapeDtypeStruct((zs, ROWS, CHUNK), jnp.int32),
            jax.ShapeDtypeStruct((CROSS, heads, *square), BF16),
            jax.ShapeDtypeStruct((heads, *square), F32),
        ),
        in_specs=[any_space] * 4 + [vmem],
        out_specs=(any_space,) * 4 + (vmem,) * 3,
        scratch_shapes=[
            pltpu.VMEM((4, heads * count, width), BF16),
            pltpu.VMEM((heads * count, width), F32),
            *[pltpu.VMEM((heads, count, width), BF16)] * 4,
            pltpu.VMEM((count, CROSS * width), F32),
            pltpu.VMEM((count, CROSS * width), BF16),
            pltpu.VMEM((heads, *square), F32),
            pltpu.VMEM((heads, *square), F32),
            *[pltpu.VMEM((4, 2, *square), F32)] * 3,
            pltpu.VMEM((CROSS, heads, *square), F32),
            pltpu.VMEM((4, heads, *square), F32),
            pltpu.VMEM((heads, *square), F32),
            *[pltpu.VMEM((4, 2, *square), F32)] * 3,
            pltpu.VMEM((2, *square), F32),
            pltpu.SemaphoreType.DMA((4,)),
            pltpu.SemaphoreType.DMA((4,)),
            pltpu.SemaphoreType.DMA((zs - 1,)),
            pltpu.SemaphoreType.DMA((zs - 1,)),
            pltpu.SemaphoreType.DMA((messages,)),
            pltpu.SemaphoreType.DMA((messages,)),
        ],
        compiler_params=pltpu.CompilerParams(
            collective_id=0, has_side_effects=True, vmem_limit_bytes=60 << 20),
        name="exchange",
    )(q, k, v, g, codes)


def local_kernel(
    scale,
    seq_ref, qh, kh, vh, gh, codes, cross, ks,
    dq_out, dk_out, dv_out,
    states, sums, mask, out_q, out_k, out_v,
):
    c = pl.program_id(0)
    heads, count, width = qh.shape
    chunks = count // CHUNK

    @pl.when(c == 0)
    def _():
        lam = []
        for n in range(chunks):
            wide = spread(codes[n], 8, INNER)
            lam.append([
                wide[:, b * CHUNK : (b + 1) * CHUNK] * factor(8 + b) for b in range(INNER)])

        @pl.loop(0, heads)
        def _(h):
            one = []
            grads = {}
            for n in range(chunks):
                rows = pl.ds(n * CHUNK, CHUNK)
                one.append(dot(vh[h, rows], kh[h, rows], TN))
                bits = [b for b in range(INNER) if n >> b & 1]
                if bits:
                    query = qh[h, rows].astype(F32)
                    wide = jnp.concatenate(
                        [(lam[n][b] * query).astype(BF16) for b in bits], axis=1)
                    res = dot(gh[h, rows], wide, TN)
                    for m, b in enumerate(bits):
                        grads[n, b] = scale * res[:, m * CHUNK : (m + 1) * CHUNK]
            base = ks[h]
            for n in range(chunks):
                total = base
                for b in range(INNER):
                    group = [i for i in range(chunks) if i >> b == (n >> b) ^ 1]
                    if n >> b & 1:
                        acc = one[group[0]]
                        for i in group[1:]:
                            acc = acc + one[i]
                        states[n, b, h] = acc.astype(BF16)
                    else:
                        acc = grads[group[0], b]
                        for i in group[1:]:
                            acc = acc + grads[i, b]
                        total = total + acc
                sums[n, h] = total.astype(BF16)

    seq = seq_ref[0]
    rows = pl.ds(c * CHUNK, CHUNK)
    here = codes[c]
    lines = [here[n : n + 1, :].astype(F32) * (factor(n) * scale) for n in range(INNER + 5)]
    s_at = lax.broadcasted_iota(jnp.int32, (CHUNK, CHUNK), 0)
    t_at = lax.broadcasted_iota(jnp.int32, (CHUNK, CHUNK), 1)
    differ = jnp.bitwise_xor(s_at, t_at)
    full = jnp.broadcast_to(lines[0], (CHUNK, CHUNK))
    for n in range(7):
        full = jnp.where(differ >= 1 << n, lines[n + 1], full)
    mask[...] = jnp.where(s_at <= t_at, full, 0.0)

    wide = spread(here, 8, INNER + CROSS)
    lam = []
    for b in range(INNER):
        on = lax.rem(jnp.right_shift(c, b), 2).astype(F32)
        lam.append(wide[:, b * CHUNK : (b + 1) * CHUNK] * (factor(8 + b) * scale * on))
    for b in range(CROSS):
        at = INNER + b
        lam.append(wide[:, at * CHUNK : (at + 1) * CHUNK]
                   * (factor(11 + b) * scale * on_bit(seq, b)))

    @pl.when(c == 0)
    def _():
        for n in range(chunks):
            for b in range(INNER):
                if not n >> b & 1:
                    states[n, b] = jnp.zeros(states.shape[2:], BF16)

    for h in range(heads):
        query, key, value, grad = qh[h, rows], kh[h, rows], vh[h, rows], gh[h, rows]
        weight_q = (mask[...] * dot(value, grad, NT)).astype(BF16)
        weight_v = (mask[...] * dot(key, query, NT)).astype(BF16)
        above = sums[c, h]
        dk = dot(weight_q, query) + dot(value, above)
        dv = dot(weight_v, grad) + dot(key, above, NT)
        grad32 = grad.astype(F32)
        dq = dot(weight_q, key, TN)
        for b in range(INNER):
            dq = dq + dot((lam[b] * grad32).astype(BF16), states[c, b, h])
        for b in range(CROSS):
            dq = dq + dot((lam[INNER + b] * grad32).astype(BF16), cross[b, h])
        at = pl.ds(h, CHUNK, stride=heads)
        out_q[at, :] = dq
        out_k[at, :] = dk
        out_v[at, :] = dv
    dq_out[...] = out_q[...].astype(BF16)
    dk_out[...] = out_k[...].astype(BF16)
    dv_out[...] = out_v[...].astype(BF16)


def local(scale, seq, qh, kh, vh, gh, codes, cross, ks):
    heads, count, width = qh.shape
    chunks = count // CHUNK
    vmem = pl.BlockSpec(memory_space=pltpu.VMEM)
    flat = jax.ShapeDtypeStruct((heads * count, width), BF16)
    return pl.pallas_call(
        functools.partial(local_kernel, scale),
        grid=(chunks,),
        out_shape=(flat, flat, flat),
        in_specs=[pl.BlockSpec(memory_space=pltpu.SMEM)] + [vmem] * 7,
        out_specs=(pl.BlockSpec((heads * CHUNK, width), lambda c: (c, 0)),) * 3,
        scratch_shapes=[
            pltpu.VMEM((chunks, INNER, heads, width, width), BF16),
            pltpu.VMEM((chunks, heads, width, width), BF16),
            pltpu.VMEM((CHUNK, CHUNK), F32),
            *[pltpu.VMEM((heads * CHUNK, width), F32)] * 3,
        ],
        compiler_params=pltpu.CompilerParams(vmem_limit_bytes=60 << 20),
        name="local",
    )(seq, qh, kh, vh, gh, codes, cross, ks)


def on_device(queries, keys, values, out_grad, level_codes):
    count, heads, width = queries.shape
    scale = width ** (-0.5)
    flat = [x.reshape(count * heads, width) for x in (queries, keys, values, out_grad)]
    qh, kh, vh, gh, codes, cross, ks = exchange(
        scale, lax.axis_size("head"), *flat, level_codes[:ROWS])
    seq = lax.axis_index("seq").astype(jnp.int32).reshape(1)
    grads = local(scale, seq, qh, kh, vh, gh, codes, cross, ks)
    return tuple(x.reshape(count, heads, width) for x in grads)


def solution(mesh):
    return jax.shard_map(
        on_device,
        mesh=mesh,
        in_specs=(
            P("seq", "head", None),
            P("seq", "head", None),
            P("seq", "head", None),
            P("seq", "head", None),
            P(None, ("seq", "head")),
        ),
        out_specs=(P("seq", "head", None), P("seq", "head", None), P("seq", "head", None)),
        check_vma=False,
    )
```

time: 191 us -> 58.1 us (0.30); the launches traced: 188 us -> 57.5 us
  matrix products: 82.7 us -> 0 us
  Pallas kernels: 0 us -> 55.6 us
  waiting for transfers between devices: 55.1 us -> 0 us
  starting transfers between devices: 24.9 us -> 0 us
  other arithmetic: 14.1 us -> 0 us
  local copies, waits for them, and re-layouts: 10.3 us -> 1.29 us
    dot_general x29 -> x0, matrix products: 82.7 us -> none  [the longest x4 43.3 us: local_head(): lax.dot_general(grad, value, inner, preferred_element_type=jnp.float32)]
    pallas_call x0 -> x2, Pallas kernels: none -> 55.6 us  [the longest x1 38.8 us: exchange(): pl.pallas_call(functools.partial(exchange_kernel, scale, zs), out_shape=(...]
    ppermute x10 -> x0, waiting for transfers between devices: 47.6 us -> none  [partner(): lax.ppermute(x, axis, [(i, i ^ 1 << apart) for i in range(lax.axis_size(a...]
    ppermute x10 -> x0, starting transfers between devices: 15.9 us -> none  [partner(): lax.ppermute(x, axis, [(i, i ^ 1 << apart) for i in range(lax.axis_size(a...]
    all_to_all x1 -> x0, starting transfers between devices: 9 us -> none  [copy_for_each(): return lax.all_to_all(copies, axis, split_axis=0, concat_axis=0, tiled=True)]
    all_to_all x1 -> x0, waiting for transfers between devices: 7.51 us -> none  [copy_for_each(): return lax.all_to_all(copies, axis, split_axis=0, concat_axis=0, tiled=True)]
    add x9 -> x0, other arithmetic: 7.26 us -> none  [the longest x4 4.86 us: on_device(): pending = pending[1:] + received[1:]]
    unnamed x55 -> x2, local copies, waits for them, and re-layouts: 7.44 us -> 0.7 us
  transfers between devices with their start and end apart: 11 -> 0, of which waited for: 9 -> 0; matrix products, arithmetic and copies ran while one was open for 45% -> 0% of each run, Pallas kernels for 0% -> 0%
where the time goes in v1:
time: 58.1 us; the launch traced here: 57.5 us
  Pallas kernels  55.6 us (96%)
  local copies, waits for them, and re-layouts  1.29 us (2%)
  between operations  0.65 us (1%)
    pallas_call x1, Pallas kernels, exchange(): pl.pallas_call(functools.partial(exchange_kernel, scale, zs), out_shape=(...  38.8 us
    pallas_call x1, Pallas kernels, local(): pl.pallas_call(functools.partial(local_kernel, scale), grid=(chunks,), ou...  16.8 us

profile of v1, /device:TPU:1, one launch (start us, length us, event | category | flops | bytes accessed | tf_op | source)
XLA Modules:
  0.0 57.5 jit_solution(13237142391312164993)
XLA Ops:
  0.6 0.0 copy-start
  0.6 0.7 %copy-done = s32[21,128]{1,0:T(8,128)S(1)} copy-done((s32[21,128]{1,0:T(8,128)S(1)}, s32[21,128]{1,0:T(8,128)}, u32[]{:S(2)}) %copy-start) | copy-done | bytes 10776
  1.3 0.6 %slice.3.codes_in = s32[16,128]{1,0:T(8,128)} slice(s32[21,128]{1,0:T(8,128)S(1)} %copy-done), slice={[0:16], [0:128]} | slice | bytes 16384 | tf_op jit(solution)/shard_map/slice | solution.py:398
  1.9 38.8 %exchange.1 = (bf16[4,1024,128]{2,1,0:T(8,128)(2,1)}, bf16[4,1024,128]{2,1,0:T(8,128)(2,1)}, bf16[4,1024,128]{2,1,0:T(8,128)(2,1)}, bf16[4,1024,128]{2,1,0:T(8,1...) custom-call(bf16[4096,128]{1,0:T(8,128)(2,1)} %bitcast.8, ...), custom_call_target="tpu_custom_call" | custom-call | tf_op jit(solution)/shard_map/exchange/pallas_call | solution.py:233
  40.7 16.8 %local.1 = (bf16[4096,128]{1,0:T(8,128)(2,1)}, bf16[4096,128]{1,0:T(8,128)(2,1)}, bf16[4096,128]{1,0:T(8,128)(2,1)}) custom-call(s32[1]{0:T(128)} %bitcast.seq_ref, bf16[4,1024,128]{2,1,0:T(8,128)(2,1)} %get-tuple-element.13.qh, bf16[4,1024,128]{2,1,0:T(8,128)(2,1)} %get-tuple-element.14.kh, bf16[4,1024,128]{2,1,0:T(8,128)(2,1)} %get-tuple-element.15.vh, ...), custom_call_target="tpu_custom_call" | custom-call | tf_op jit(solution)/shard_map/local/pallas_call | solution.py:376
Async XLA Ops:
  0.6 0.7 %copy-start = (s32[21,128]{1,0:T(8,128)S(1)}, s32[21,128]{1,0:T(8,128)}, u32[]{:S(2)}) copy-start(s32[21,128]{1,0:T(8,128)} %param.9) | copy-start | bytes 32260

commit v2 on v1

v2 whole, which is shorter than its diff:
```python
import functools

import jax
import jax.numpy as jnp
from jax import lax
from jax.experimental import pallas as pl
from jax.experimental.pallas import tpu as pltpu
from jax.sharding import PartitionSpec as P

MESH = pl.DeviceIdType.MESH
F32 = jnp.float32
BF16 = jnp.bfloat16
CHUNK = 128
INNER = 3
CROSS = 5
ROWS = 16
PARTNERS = (1, 2, 6, 8, 24)

NN = (((1,), (0,)), ((), ()))
NT = (((1,), (1,)), ((), ()))
TN = (((0,), (0,)), ((), ()))


def dot(a, b, dims=NN):
    return lax.dot_general(a, b, dims, preferred_element_type=F32)


def factor(level):
    return 2.0 ** (-0.5 * max(level - 1, 0)) / 16.0


def on_bit(index, bit):
    return lax.rem(jnp.right_shift(index, bit), 2).astype(F32)


def spread(codes, first, count):
    rows = lax.broadcasted_iota(jnp.int32, (codes.shape[0], count * CHUNK), 0)
    cols = lax.broadcasted_iota(jnp.int32, (codes.shape[0], count * CHUNK), 1)
    pick = (rows == first + jnp.right_shift(cols, 7)).astype(F32).astype(BF16)
    return dot(codes.astype(F32).astype(BF16), pick, TN)


def split_heads(flat, tmp, out):
    heads, count, _ = out.shape
    tmp[...] = flat[...].astype(F32)
    for h in range(heads):
        out[h] = tmp[pl.ds(h, count, stride=heads), :].astype(BF16)


def chunk(n, count=1):
    return pl.ds(n * CHUNK, count * CHUNK)


PAIRS = (
    (0, (0, 1), (1, 2)), (0, (2, 3), (3, 4)), (0, (4, 5), (5, 6)), (0, (6, 7), (7, 8)),
    (1, (0, 2), (2, 4)), (1, (4, 6), (6, 8)),
    (2, (0, 4), (4, 8)),
)


def exchange_kernel(
    scale, zs,
    q_in, k_in, v_in, g_in, codes_in,
    dq_out, dk_out, dv_out, ks_out, inner_out,
    flat, tmp, qh, kh, vh, gh, gt, lam, codes,
    one, states, inner, mask, dq, flat_k, flat_v, cross,
    state, r_state, tot, r_tot, r_found,
    level, r_level, r_level0, down, r_down, mid, r_mid,
    in_sem, out_sem, code_send, code_recv, send, recv,
):
    seq = lax.axis_index("seq")
    z = lax.axis_index("head")
    mine = 2 * lax.rem(seq, 2)
    theirs = 2 - mine
    heads, count, width = qh.shape
    chunks = count // CHUNK
    subs = range(4)
    half = CHUNK // 2
    partner = [jnp.bitwise_xor(seq, p) for p in PARTNERS]

    barrier = pltpu.get_barrier_semaphore()
    for d in range(1, zs):
        pl.semaphore_signal(
            barrier, inc=1, device_id=(seq, lax.rem(z + d, zs)), device_id_type=MESH)
    for p in partner:
        pl.semaphore_signal(barrier, inc=1, device_id=(p, z), device_id_type=MESH)

    loads = [
        pltpu.make_async_copy(src, flat.at[i], in_sem.at[i])
        for i, src in enumerate((k_in, v_in, q_in, g_in))
    ]
    here = pltpu.make_async_copy(codes_in.at[pl.ds(0, ROWS)], codes.at[z], in_sem.at[4])
    for c in loads:
        c.start()
    here.start()

    sent = []

    def remote(src, dst, to):
        n = len(sent)
        c = pltpu.make_async_remote_copy(
            src_ref=src, dst_ref=dst, send_sem=send.at[n], recv_sem=recv.at[n],
            device_id=(partner[to], z), device_id_type=MESH)
        sent.append(c)
        c.start()
        return c

    outs = []

    def put(src, dst):
        c = pltpu.make_async_copy(src, dst, out_sem.at[len(outs)])
        c.start()
        outs.append(c)

    loads[0].wait()
    split_heads(flat.at[0], tmp, kh)
    loads[1].wait()
    split_heads(flat.at[1], tmp, vh)
    here.wait()

    @pl.loop(0, heads)
    def _(h):
        for n in range(chunks):
            one[n] = dot(vh[h, chunk(n)], kh[h, chunk(n)], TN)
        total = one[0]
        for n in range(1, chunks):
            total = total + one[n]
        state[h] = total
        for m, (_, (lo, hi), _) in enumerate(PAIRS):
            acc = one[lo]
            for n in range(lo + 1, hi):
                acc = acc + one[n]
            states[m, h] = acc.astype(BF16)

    pl.semaphore_wait(barrier, len(partner) + zs - 1)
    codes_sent = []
    for d in range(1, zs):
        c = pltpu.make_async_remote_copy(
            src_ref=codes_in.at[pl.ds(0, ROWS)], dst_ref=codes.at[z],
            send_sem=code_send.at[d - 1], recv_sem=code_recv.at[d - 1],
            device_id=(seq, lax.rem(z + d, zs)), device_id_type=MESH)
        c.start()
        codes_sent.append(c)
    s_their = remote(state.at[pl.ds(theirs, 2)], r_state.at[pl.ds(theirs, 2)], 0)
    s_mine = remote(state.at[pl.ds(mine, 2)], r_state.at[pl.ds(mine, 2)], 0)

    def part(ref, s, *lead):
        return ref[(*lead, mine + s // 2, pl.ds(s % 2 * half, half))]

    loads[2].wait()
    split_heads(flat.at[2], tmp, qh)

    s_their.wait_recv()
    up = [[]]
    for s in subs:
        tot[0, s] = part(state, s) + part(r_state, s)
        up[0].append(remote(tot.at[0, s], r_tot.at[0, s], 1))

    loads[3].wait()
    split_heads(flat.at[3], tmp, gh)

    @pl.loop(0, heads)
    def _(h):
        for n in range(chunks):
            gt[h, :, chunk(n)] = gh[h, chunk(n)].T

    def step_up(p):
        up.append([])
        for s in subs:
            up[p - 1][s].wait_recv()
            tot[p, s] = tot[p - 1, s] + r_tot[p - 1, s]
            up[p].append(remote(tot.at[p, s], r_tot.at[p, s], p + 1))

    def weights(first, number):
        @pl.loop(0, zs)
        def _(c):
            wide = spread(codes[c], 8 + first, number)
            for b in range(number):
                at = first + b
                value = factor(8 + at)
                if at >= INNER:
                    value = value * on_bit(seq, at - INNER)
                lam[chunk(c), chunk(at)] = wide[:, b * CHUNK : (b + 1) * CHUNK] * value

    def level_grad(b, first):
        @pl.loop(0, 2)
        def _(i):
            h = first + i
            wide = (lam[:, chunk(INNER + b)] * qh[h].astype(F32)).astype(BF16)
            level[b, h] = scale * dot(gt[h], wide)

    halves = [None] * CROSS

    def both_grads(b):
        level_grad(b, theirs)
        halves[b] = remote(
            level.at[b, pl.ds(theirs, 2)], r_level.at[b - 1, pl.ds(theirs, 2)], 0)
        level_grad(b, mine)

    for c in codes_sent:
        c.wait_recv()
    weights(INNER + 4, 1)
    both_grads(4)
    step_up(1)
    weights(INNER, 4)
    level_grad(3, theirs)
    halves[3] = remote(level.at[3, pl.ds(theirs, 2)], r_level.at[2, pl.ds(theirs, 2)], 0)
    halves[4].wait_recv()
    now = []
    for s in subs:
        down[0, s] = part(level, s, 4) + part(r_level, s, 3)
        now.append(remote(down.at[0, s], r_down.at[0, s], 4))
    level_grad(3, mine)
    both_grads(2)
    both_grads(1)
    level_grad(0, theirs)
    level_grad(0, mine)
    whole = remote(level.at[0], r_level0, 0)
    step_up(2)

    def masks():
        s_at = lax.broadcasted_iota(jnp.int32, (CHUNK, CHUNK), 0)
        t_at = lax.broadcasted_iota(jnp.int32, (CHUNK, CHUNK), 1)
        differ = jnp.bitwise_xor(s_at, t_at)

        @pl.loop(0, chunks)
        def _(n):
            full = jnp.zeros((CHUNK, CHUNK), F32)
            for m in range(8):
                line = codes[n, m : m + 1, :].astype(F32) * (factor(m) * scale)
                if m == 0:
                    full = jnp.broadcast_to(line, (CHUNK, CHUNK))
                else:
                    full = jnp.where(differ >= 1 << (m - 1), line, full)
            mask[n] = jnp.where(s_at <= t_at, full, 0.0)

    def inner_grads():
        weights(0, INNER)
        inner[7] = jnp.zeros(inner.shape[1:], F32)

        @pl.loop(0, heads)
        def _(h):
            found = []
            for b, _, (lo, hi) in PAIRS:
                query = qh[h, chunk(lo, hi - lo)].astype(F32)
                wide = (lam[chunk(lo, hi - lo), chunk(b)] * query).astype(BF16)
                found.append(scale * dot(gt[h, :, chunk(lo, hi - lo)], wide))
            for n in range(chunks - 1):
                parts = [found[m] for m, (_, (lo, hi), _) in enumerate(PAIRS) if lo <= n < hi]
                acc = parts[0]
                for x in parts[1:]:
                    acc = acc + x
                inner[n, h] = acc

    def diagonal(h, first, number):
        for n in range(first, first + number):
            rows = chunk(n)
            query, key, value, grad = qh[h, rows], kh[h, rows], vh[h, rows], gh[h, rows]
            weight_q = (mask[n] * dot(value, grad, NT)).astype(BF16)
            weight_v = (mask[n] * dot(key, query, NT)).astype(BF16)
            at = pl.ds(n * CHUNK * heads + h, CHUNK, stride=heads)
            flat_k[at, :] = dot(weight_q, query)
            flat_v[at, :] = dot(weight_v, grad)
            total = dot(weight_q, key, TN)
            grad32 = grad.astype(F32) * scale
            for m, (b, _, (lo, hi)) in enumerate(PAIRS):
                if lo <= n < hi:
                    wide = (lam[rows, chunk(b)] * grad32).astype(BF16)
                    total = total + dot(wide, states[m, h])
            dq[h, rows] = total

    def put_keys():
        put(flat_k, dk_out)
        put(flat_v, dv_out)
        put(inner, inner_out)

    def across(h):
        @pl.loop(0, 2)
        def _(i):
            rows = pl.ds(i * (count // 2), count // 2)
            grad32 = gh[h, rows].astype(F32) * scale
            wide = jnp.concatenate(
                [(lam[rows, chunk(INNER + b)] * grad32).astype(BF16) for b in range(CROSS)],
                axis=1)
            matrix = jnp.concatenate([cross[b, h] for b in range(CROSS)], axis=0)
            at = pl.ds(i * (heads * count // 2) + h, count // 2, stride=heads)
            tmp[at, :] = dq[h, rows] + dot(wide, matrix)

    def put_queries():
        flat[0] = tmp[...].astype(BF16)
        put(flat.at[0], dq_out)

    work = [masks, inner_grads]
    for h in range(heads):
        work.append(functools.partial(diagonal, h, 0, 4))
        work.append(functools.partial(diagonal, h, 4, 4))
    work.append(put_keys)
    work_after = [functools.partial(across, h) for h in range(heads)] + [put_queries]

    def do(queue, number=1):
        for _ in range(number):
            if queue:
                queue.pop(0)()

    found = []
    for n, b in enumerate((3, 2, 1)):
        halves[b].wait_recv()
        after = []
        for s in subs:
            now[s].wait_recv()
            value = r_down[n, s]
            if n:
                value = value + mid[n - 1, s]
            mid[n, s] = value
            down[n + 1, s] = value + part(level, s, b) + part(r_level, s, b - 1)
            after.append(remote(down.at[n + 1, s], r_down.at[n + 1, s], b))
            do(work)
        now = after
        if n == 0:
            step_up(3)
            for p in range(3):
                found.append(remote(r_tot.at[p], r_found.at[p], 0))
        if n == 1:
            for s in subs:
                up[3][s].wait_recv()
            found.append(remote(r_tot.at[3], r_found.at[3], 0))
    do(work, len(work))

    s_mine.wait_recv()
    for h in range(heads):
        cross[0, h] = r_state[h].astype(BF16)
    for p in range(4):
        found[p].wait_recv()
        for s in subs:
            rows = pl.ds(s % 2 * half, half)
            cross[p + 1, mine + s // 2, rows] = r_tot[p, s].astype(BF16)
            cross[p + 1, theirs + s // 2, rows] = r_found[p, s].astype(BF16)
    last = []
    for s in subs:
        now[s].wait_recv()
        mid[3, s] = mid[2, s] + r_down[3, s]
        last.append(remote(mid.at[3, s], r_mid.at[s], 0))
        do(work_after)
    do(work_after, len(work_after))

    whole.wait_recv()
    for s in subs:
        last[s].wait_recv()
        rows = pl.ds(s % 2 * half, half)
        i = s // 2
        ks_out[mine + i, rows] = mid[3, s] + r_level0[mine + i, rows]
        ks_out[theirs + i, rows] = r_mid[s] + r_level0[theirs + i, rows]

    for c in sent + codes_sent:
        c.wait_send()
    for c in outs:
        c.wait()


def exchange(scale, zs, heads, q, k, v, g, codes):
    count, width = q.shape[0] // heads, q.shape[1]
    chunks = count // CHUNK
    square = (width, width)
    piece = (4, 4, CHUNK // 2, width)
    any_space = pl.BlockSpec(memory_space=pl.ANY)
    vmem = pl.BlockSpec(memory_space=pltpu.VMEM)
    messages = 2 + 16 + 4 + 4 + 1 + 16 + 4
    return pl.pallas_call(
        functools.partial(exchange_kernel, scale, zs),
        out_shape=(
            jax.ShapeDtypeStruct((heads * count, width), BF16),
            jax.ShapeDtypeStruct((heads * count, width), F32),
            jax.ShapeDtypeStruct((heads * count, width), F32),
            jax.ShapeDtypeStruct((heads, *square), F32),
            jax.ShapeDtypeStruct((chunks, heads, *square), F32),
        ),
        in_specs=[any_space] * 5,
        out_specs=(any_space, any_space, any_space, vmem, any_space),
        scratch_shapes=[
            pltpu.VMEM((4, heads * count, width), BF16),
            pltpu.VMEM((heads * count, width), F32),
            *[pltpu.VMEM((heads, count, width), BF16)] * 4,
            pltpu.VMEM((heads, width, count), BF16),
            pltpu.VMEM((count, (INNER + CROSS) * width), F32),
            pltpu.VMEM((zs, ROWS, CHUNK), jnp.int32),
            pltpu.VMEM((chunks, *square), F32),
            pltpu.VMEM((len(PAIRS), heads, *square), BF16),
            pltpu.VMEM((chunks, heads, *square), F32),
            pltpu.VMEM((chunks, CHUNK, CHUNK), F32),
            pltpu.VMEM((heads, count, width), F32),
            pltpu.VMEM((heads * count, width), F32),
            pltpu.VMEM((heads * count, width), F32),
            pltpu.VMEM((CROSS, heads, *square), BF16),
            pltpu.VMEM((heads, *square), F32),
            pltpu.VMEM((heads, *square), F32),
            *[pltpu.VMEM(piece, F32)] * 3,
            pltpu.VMEM((CROSS, heads, *square), F32),
            pltpu.VMEM((4, heads, *square), F32),
            pltpu.VMEM((heads, *square), F32),
            *[pltpu.VMEM(piece, F32)] * 3,
            pltpu.VMEM(piece[1:], F32),
            pltpu.SemaphoreType.DMA((5,)),
            pltpu.SemaphoreType.DMA((4,)),
            pltpu.SemaphoreType.DMA((zs - 1,)),
            pltpu.SemaphoreType.DMA((zs - 1,)),
            pltpu.SemaphoreType.DMA((messages,)),
            pltpu.SemaphoreType.DMA((messages,)),
        ],
        compiler_params=pltpu.CompilerParams(
            collective_id=0, has_side_effects=True, vmem_limit_bytes=EXCHANGE_VMEM),
        name="exchange",
    )(q, k, v, g, codes)


EXCHANGE_VMEM = 60 << 20


def finish_kernel(k_in, v_in, dq_in, dk_in, dv_in, ks, inner, dq_out, dk_out, dv_out):
    heads = ks.shape[0]
    row = lax.broadcasted_iota(jnp.int32, (16, CHUNK), 0)
    keep = [
        (lax.rem(row, heads) == h).astype(F32).astype(BF16).reshape(1, 16, CHUNK)
        for h in range(heads)
    ]
    dq_out[...] = dq_in[...]
    steps = inner.shape[0]
    rows = heads * CHUNK
    for n in range(steps):
        at = pl.ds(n * rows, rows)
        total = [(ks[h] + inner[n, h]).astype(BF16) for h in range(heads)]

        def by_head(ref):
            x = ref[at, :].reshape(rows // 16, 16, CHUNK)
            return jnp.concatenate([(x * keep[h]).reshape(rows, CHUNK) for h in range(heads)], axis=1)

        dk = dot(by_head(v_in), jnp.concatenate(total, axis=0))
        dk_out[at, :] = (dk_in[at, :] + dk).astype(BF16)
        dv = dot(by_head(k_in), jnp.concatenate([x.T for x in total], axis=0))
        dv_out[at, :] = (dv_in[at, :] + dv).astype(BF16)


def finish(k, v, dq, dk, dv, ks, inner, steps=1):
    chunks, heads, width, _ = inner.shape
    block = pl.BlockSpec((steps * heads * CHUNK, width), lambda c: (c, 0))
    flat = jax.ShapeDtypeStruct(k.shape, BF16)
    return pl.pallas_call(
        finish_kernel,
        grid=(chunks // steps,),
        out_shape=(flat, flat, flat),
        in_specs=[block] * 5 + [
            pl.BlockSpec(memory_space=pltpu.VMEM),
            pl.BlockSpec((steps, heads, width, width), lambda c: (c, 0, 0, 0)),
        ],
        out_specs=(block,) * 3,
        compiler_params=pltpu.CompilerParams(vmem_limit_bytes=60 << 20),
        name="finish",
    )(k, v, dq, dk, dv, ks, inner)


def on_device(queries, keys, values, out_grad, level_codes):
    count, heads, width = queries.shape
    scale = width ** (-0.5)
    q, k, v, g = [x.reshape(count * heads, width) for x in (queries, keys, values, out_grad)]
    dq, dk, dv, ks, inner = exchange(
        scale, lax.axis_size("head"), heads, q, k, v, g, level_codes)
    grads = finish(k, v, dq, dk, dv, ks, inner)
    return tuple(x.reshape(count, heads, width) for x in grads)


def solution(mesh):
    return jax.shard_map(
        on_device,
        mesh=mesh,
        in_specs=(
            P("seq", "head", None),
            P("seq", "head", None),
            P("seq", "head", None),
            P("seq", "head", None),
            P(None, ("seq", "head")),
        ),
        out_specs=(P("seq", "head", None), P("seq", "head", None), P("seq", "head", None)),
        check_vma=False,
    )
```

time: 58.1 us -> 51.8 us (0.89)
  Pallas kernels: 55.6 us -> 50.9 us
  local copies, waits for them, and re-layouts: 1.29 us -> 0 us
    pallas_call x1, Pallas kernels: 16.8 us -> 8.88 us  [finish(): pl.pallas_call(finish_kernel, grid=(chunks // steps,), out_shape=(flat, f...]
    pallas_call x1, Pallas kernels: 38.8 us -> 42.1 us  [exchange(): pl.pallas_call(functools.partial(exchange_kernel, scale, zs), out_shape=(...]
    unnamed x2 -> x0, local copies, waits for them, and re-layouts: 0.7 us -> none
    slice x1 -> x0, local copies, waits for them, and re-layouts: 0.6 us -> none  [on_device(): level_codes[:ROWS]]
where the time goes in v2:
time: 51.8 us; the launch traced here: 51.6 us
  Pallas kernels  50.9 us (98%)
  between operations  0.64 us (1%)
    pallas_call x1, Pallas kernels, exchange(): pl.pallas_call(functools.partial(exchange_kernel, scale, zs), out_shape=(...  42.1 us
    pallas_call x1, Pallas kernels, finish(): pl.pallas_call(finish_kernel, grid=(chunks // steps,), out_shape=(flat, f...  8.88 us

profile of v2, /device:TPU:1, one launch (start us, length us, event | category | flops | bytes accessed | tf_op | source)
XLA Modules:
  0.0 51.6 jit_solution(17005657144140494074)
XLA Ops:
  0.6 42.1 %exchange.1 = (bf16[4096,128]{1,0:T(8,128)(2,1)}, f32[4096,128]{1,0:T(8,128)}, f32[4096,128]{1,0:T(8,128)}, f32[4,128,128]{2,1,0:T(8,128)}, f32[8,4,128,128]{3,2,1,0:T(8,128)}) custom-call(bf16[4096,128]{1,0:T(8,128)(2,1)} %bitcast.11, bf16[4096,128]{1,0:T(8,128)(2,1)} %bitcast.7, bf16[4096,128]{1,0:T(8,128)(2,1)} %bitcast.9, bf16[4096,128]{1,0:T(8,128)(2,1)} %bitcast.12, ...), custom_call_target="tpu_custom_call" | custom-call | tf_op jit(solution)/shard_map/exchange/pallas_call | solution.py:368
  42.7 8.9 %finish.1 = (bf16[4096,128]{1,0:T(8,128)(2,1)}, bf16[4096,128]{1,0:T(8,128)(2,1)}, bf16[4096,128]{1,0:T(8,128)(2,1)}) custom-call(bf16[4096,128]{1,0:T(8,128)(2,1)} %bitcast.8, bf16[4096,128]{1,0:T(8,128)(2,1)} %bitcast.10, bf16[4096,128]{1,0:T(8,128)(2,1)} %get-tuple-element.11.dq_in, f32[4096,128]{1,0:T(8,128)} %get-tuple-element.12.dk_in, ...), custom_call_target="tpu_custom_call" | custom-call | tf_op jit(solution)/shard_map/finish/pallas_call | solution.py:446

commit v3 on v2

v3 whole, which is shorter than its diff:
```python
import functools

import jax
import jax.numpy as jnp
from jax import lax
from jax.experimental import pallas as pl
from jax.experimental.pallas import tpu as pltpu
from jax.sharding import PartitionSpec as P

MESH = pl.DeviceIdType.MESH
F32 = jnp.float32
BF16 = jnp.bfloat16
CHUNK = 128
INNER = 3
CROSS = 5
ROWS = 16
PARTNERS = (1, 2, 6, 8, 24)

NN = (((1,), (0,)), ((), ()))
NT = (((1,), (1,)), ((), ()))
TN = (((0,), (0,)), ((), ()))


def dot(a, b, dims=NN):
    return lax.dot_general(a, b, dims, preferred_element_type=F32)


def factor(level):
    return 2.0 ** (-0.5 * max(level - 1, 0)) / 16.0


def on_bit(index, bit):
    return lax.rem(jnp.right_shift(index, bit), 2).astype(F32)


def spread(codes, first, count):
    rows = lax.broadcasted_iota(jnp.int32, (codes.shape[0], count * CHUNK), 0)
    cols = lax.broadcasted_iota(jnp.int32, (codes.shape[0], count * CHUNK), 1)
    pick = (rows == first + jnp.right_shift(cols, 7)).astype(F32).astype(BF16)
    return dot(codes.astype(F32).astype(BF16), pick, TN)


def split_heads(flat, tmp, out):
    heads, count, _ = out.shape
    tmp[...] = flat[...].astype(F32)
    for h in range(heads):
        out[h] = tmp[pl.ds(h, count, stride=heads), :].astype(BF16)


def chunk(n, count=1):
    return pl.ds(n * CHUNK, count * CHUNK)


def total_of(items):
    items = list(items)
    acc = items[0]
    for x in items[1:]:
        acc = acc + x
    return acc


PAIRS = (
    (0, (0, 1), (1, 2)), (0, (2, 3), (3, 4)), (0, (4, 5), (5, 6)), (0, (6, 7), (7, 8)),
    (1, (0, 2), (2, 4)), (1, (4, 6), (6, 8)),
    (2, (0, 4), (4, 8)),
)


def exchange_kernel(
    scale, zs,
    q_in, k_in, v_in, g_in, codes_in,
    dq_out, dk_out, dv_out,
    flat, tmp, qh, kh, vh, gh, gt, lam, codes,
    one, states, inner, inner_t, mask, weight, dq, dk, dv, flat_k, flat_v, cross, ks,
    state, r_state, tot, r_tot, r_found,
    level, r_level, r_level0, down, r_down, mid, r_mid,
    in_sem, out_sem, code_send, code_recv, send, recv,
):
    seq = lax.axis_index("seq")
    z = lax.axis_index("head")
    mine = 2 * lax.rem(seq, 2)
    theirs = 2 - mine
    heads, count, width = qh.shape
    chunks = count // CHUNK
    subs = range(4)
    half = CHUNK // 2
    partner = [jnp.bitwise_xor(seq, p) for p in PARTNERS]

    barrier = pltpu.get_barrier_semaphore()
    for d in range(1, zs):
        pl.semaphore_signal(
            barrier, inc=1, device_id=(seq, lax.rem(z + d, zs)), device_id_type=MESH)
    for p in partner:
        pl.semaphore_signal(barrier, inc=1, device_id=(p, z), device_id_type=MESH)

    loads = [
        pltpu.make_async_copy(src, flat.at[i], in_sem.at[i])
        for i, src in enumerate((k_in, v_in, q_in, g_in))
    ]
    here = pltpu.make_async_copy(codes_in.at[pl.ds(0, ROWS)], codes.at[z], in_sem.at[4])
    for c in loads:
        c.start()
    here.start()

    sent = []

    def remote(src, dst, to):
        n = len(sent)
        c = pltpu.make_async_remote_copy(
            src_ref=src, dst_ref=dst, send_sem=send.at[n], recv_sem=recv.at[n],
            device_id=(partner[to], z), device_id_type=MESH)
        sent.append(c)
        c.start()
        return c

    outs = []

    def put(src, dst):
        c = pltpu.make_async_copy(src, dst, out_sem.at[len(outs)])
        c.start()
        outs.append(c)

    loads[0].wait()
    split_heads(flat.at[0], tmp, kh)
    loads[1].wait()
    split_heads(flat.at[1], tmp, vh)
    here.wait()

    @pl.loop(0, heads // 2)
    def _(pair):
        for i in range(2):
            h = 2 * pair + i
            for n in range(chunks):
                one[i, n] = dot(vh[h, chunk(n)], kh[h, chunk(n)], TN)
            state[h] = total_of(one[i, n] for n in range(chunks))
            for m, (b, (lo, hi), _) in enumerate(PAIRS):
                acc = total_of(one[i, n] for n in range(lo, hi))
                states[m, h] = (acc * (scale * factor(8 + b))).astype(BF16)

    pl.semaphore_wait(barrier, len(partner) + zs - 1)
    codes_sent = []
    for d in range(1, zs):
        c = pltpu.make_async_remote_copy(
            src_ref=codes_in.at[pl.ds(0, ROWS)], dst_ref=codes.at[z],
            send_sem=code_send.at[d - 1], recv_sem=code_recv.at[d - 1],
            device_id=(seq, lax.rem(z + d, zs)), device_id_type=MESH)
        c.start()
        codes_sent.append(c)
    s_their = remote(state.at[pl.ds(theirs, 2)], r_state.at[pl.ds(theirs, 2)], 0)
    s_mine = remote(state.at[pl.ds(mine, 2)], r_state.at[pl.ds(mine, 2)], 0)

    def part(ref, s, *lead):
        return ref[(*lead, mine + s // 2, pl.ds(s % 2 * half, half))]

    loads[3].wait()
    split_heads(flat.at[3], tmp, gh)

    s_their.wait_recv()
    up = [[]]
    for s in subs:
        tot[0, s] = part(state, s) + part(r_state, s)
        up[0].append(remote(tot.at[0, s], r_tot.at[0, s], 1))

    loads[2].wait()
    split_heads(flat.at[2], tmp, qh)
    for h in range(heads):
        for n in range(chunks):
            gt[h, :, chunk(n)] = gh[h, chunk(n)].T

    def step_up(p):
        up.append([])
        for s in subs:
            up[p - 1][s].wait_recv()
            tot[p, s] = tot[p - 1, s] + r_tot[p - 1, s]
            up[p].append(remote(tot.at[p, s], r_tot.at[p, s], p + 1))

    def spread_codes(first, number):
        for c in range(chunks):
            lam[chunk(c), chunk(first, number)] = spread(codes[c], 8 + first, number).astype(BF16)

    def level_grads(bits, h):
        wide = jnp.concatenate([lam[:, chunk(INNER + b)] * qh[h] for b in bits], axis=1)
        result = dot(gt[h], wide)
        for i, b in enumerate(bits):
            level[b, h] = (scale * factor(11 + b) * on_bit(seq, b)) * result[
                :, i * CHUNK : (i + 1) * CHUNK]

    halves = [None] * CROSS

    def send_half(b):
        halves[b] = remote(
            level.at[b, pl.ds(theirs, 2)], r_level.at[b - 1, pl.ds(theirs, 2)], 0)

    for c in codes_sent:
        c.wait_recv()
    spread_codes(INNER + 3, 2)
    for i in range(2):
        level_grads((3, 4), theirs + i)
    send_half(4)
    send_half(3)
    for i in range(2):
        level_grads((3, 4), mine + i)
    step_up(1)
    spread_codes(0, INNER + 3)
    halves[4].wait_recv()
    now = []
    for s in subs:
        down[0, s] = part(level, s, 4) + part(r_level, s, 3)
        now.append(remote(down.at[0, s], r_down.at[0, s], 4))
    for i in range(2):
        level_grads((0, 1, 2), theirs + i)
    send_half(2)
    send_half(1)
    for i in range(2):
        level_grads((0, 1, 2), mine + i)
    whole = remote(level.at[0], r_level0, 0)
    step_up(2)

    def masks():
        s_at = lax.broadcasted_iota(jnp.int32, (CHUNK, CHUNK), 0)
        t_at = lax.broadcasted_iota(jnp.int32, (CHUNK, CHUNK), 1)
        differ = jnp.bitwise_xor(s_at, t_at)

        @pl.loop(0, chunks)
        def _(n):
            full = jnp.zeros((CHUNK, CHUNK), F32)
            for m in range(8):
                line = codes[n, m : m + 1, :].astype(F32) * (factor(m) * scale)
                if m == 0:
                    full = jnp.broadcast_to(line, (CHUNK, CHUNK))
                else:
                    full = jnp.where(differ >= 1 << (m - 1), line, full)
            mask[n] = jnp.where(s_at <= t_at, full, 0.0)

    def inner_grads(first):
        for h in range(first, first + 2):
            found = []
            for b, _, (lo, hi) in PAIRS:
                rows = chunk(lo, hi - lo)
                wide = lam[rows, chunk(b)] * qh[h, rows]
                found.append((scale * factor(8 + b)) * dot(gt[h, :, rows], wide))
            for n in range(chunks - 1):
                acc = total_of(
                    found[m] for m, (_, (lo, hi), _) in enumerate(PAIRS) if lo <= n < hi)
                value = acc.astype(BF16)
                inner[n, h] = value
                inner_t[n, h] = value.T

    def first_stage(u):
        h, start = u // 2, u % 2 * 4
        for i in range(4):
            rows = chunk(start + i)
            weights = mask[start + i]
            weight[u % 2, i, 0] = (weights * dot(vh[h, rows], gh[h, rows], NT)).astype(BF16)
            weight[u % 2, i, 1] = (weights * dot(kh[h, rows], qh[h, rows], NT)).astype(BF16)

    def second_stage(u):
        h, start = u // 2, u % 2 * 4
        for i in range(4):
            n = start + i
            rows = chunk(n)
            query, key, value, grad = qh[h, rows], kh[h, rows], vh[h, rows], gh[h, rows]
            weight_q, weight_v = weight[u % 2, i, 0], weight[u % 2, i, 1]
            if n < chunks - 1:
                dk[h, rows] = dot(
                    jnp.concatenate([weight_q, value], axis=1),
                    jnp.concatenate([query, inner[n, h]], axis=0))
                dv[h, rows] = dot(
                    jnp.concatenate([weight_v, key], axis=1),
                    jnp.concatenate([grad, inner_t[n, h]], axis=0))
            else:
                dk[h, rows] = dot(weight_q, query)
                dv[h, rows] = dot(weight_v, grad)
            left, right = [weight_q.T], [key]
            for m, (b, _, (lo, hi)) in enumerate(PAIRS):
                if lo <= n < hi:
                    left.append(lam[rows, chunk(b)] * grad)
                    right.append(states[m, h])
            dq[h, rows] = dot(jnp.concatenate(left, axis=1), jnp.concatenate(right, axis=0))

    def diagonal(u):
        if u > 0:
            second_stage(u - 1)
        if u < 8:
            first_stage(u)

    def across(h):
        wide = jnp.concatenate([lam[:, chunk(INNER + b)] * gh[h] for b in range(CROSS)], axis=1)
        matrix = jnp.concatenate([cross[b, h] for b in range(CROSS)], axis=0)
        tmp[pl.ds(h, count, stride=heads), :] = dq[h] + dot(wide, matrix)

    def put_queries():
        flat[0] = tmp[...].astype(BF16)
        put(flat.at[0], dq_out)

    def finish(h):
        at = pl.ds(h, count, stride=heads)
        flat_k[at, :] = dk[h] + dot(vh[h], ks[h])
        flat_v[at, :] = dv[h] + dot(kh[h], ks[h], NT)

    work = [masks, functools.partial(inner_grads, 0), functools.partial(inner_grads, 2)]
    work += [functools.partial(diagonal, u) for u in range(9)]

    def do(number=1):
        for _ in range(number):
            if work:
                work.pop(0)()

    found = []
    for n, b in enumerate((3, 2, 1)):
        halves[b].wait_recv()
        after = []
        for s in subs:
            now[s].wait_recv()
            value = r_down[n, s]
            if n:
                value = value + mid[n - 1, s]
            mid[n, s] = value
            down[n + 1, s] = value + part(level, s, b) + part(r_level, s, b - 1)
            after.append(remote(down.at[n + 1, s], r_down.at[n + 1, s], b))
            do()
        now = after
        if n == 0:
            step_up(3)
            for p in range(3):
                found.append(remote(r_tot.at[p], r_found.at[p], 0))
        if n == 1:
            for s in subs:
                up[3][s].wait_recv()
            found.append(remote(r_tot.at[3], r_found.at[3], 0))
    do(len(work))

    s_mine.wait_recv()
    for h in range(heads):
        cross[0, h] = ((scale * factor(11)) * on_bit(seq, 0) * r_state[h]).astype(BF16)
    for p in range(4):
        found[p].wait_recv()
        value = (scale * factor(12 + p)) * on_bit(seq, p + 1)
        for s in subs:
            rows = pl.ds(s % 2 * half, half)
            cross[p + 1, mine + s // 2, rows] = (value * r_tot[p, s]).astype(BF16)
            cross[p + 1, theirs + s // 2, rows] = (value * r_found[p, s]).astype(BF16)
    for h in range(heads):
        across(h)
    put_queries()

    last = []
    whole.wait_recv()
    for s in subs:
        now[s].wait_recv()
        mid[3, s] = mid[2, s] + r_down[3, s]
        last.append(remote(mid.at[3, s], r_mid.at[s], 0))
        rows = pl.ds(s % 2 * half, half)
        ks[mine + s // 2, rows] = (mid[3, s] + part(r_level0, s)).astype(BF16)
        if s % 2:
            finish(mine + s // 2)
    for s in subs:
        last[s].wait_recv()
        rows = pl.ds(s % 2 * half, half)
        ks[theirs + s // 2, rows] = (r_mid[s] + r_level0[theirs + s // 2, rows]).astype(BF16)
    for i in range(2):
        finish(theirs + i)
    flat[1] = flat_k[...].astype(BF16)
    put(flat.at[1], dk_out)
    flat[2] = flat_v[...].astype(BF16)
    put(flat.at[2], dv_out)

    for c in sent + codes_sent:
        c.wait_send()
    for c in outs:
        c.wait()


def exchange(scale, zs, heads, q, k, v, g, codes):
    count, width = q.shape[0] // heads, q.shape[1]
    chunks = count // CHUNK
    square = (width, width)
    piece = (4, 4, CHUNK // 2, width)
    any_space = pl.BlockSpec(memory_space=pl.ANY)
    messages = 2 + 16 + 4 + 4 + 1 + 16 + 4
    flat = jax.ShapeDtypeStruct((heads * count, width), BF16)
    return pl.pallas_call(
        functools.partial(exchange_kernel, scale, zs),
        out_shape=(flat,) * 3,
        in_specs=[any_space] * 5,
        out_specs=(any_space,) * 3,
        scratch_shapes=[
            pltpu.VMEM((4, heads * count, width), BF16),
            pltpu.VMEM((heads * count, width), F32),
            *[pltpu.VMEM((heads, count, width), BF16)] * 4,
            pltpu.VMEM((heads, width, count), BF16),
            pltpu.VMEM((count, (INNER + CROSS) * width), BF16),
            pltpu.VMEM((zs, ROWS, CHUNK), jnp.int32),
            pltpu.VMEM((2, chunks, *square), F32),
            pltpu.VMEM((len(PAIRS), heads, *square), BF16),
            *[pltpu.VMEM((chunks - 1, heads, *square), BF16)] * 2,
            pltpu.VMEM((chunks, CHUNK, CHUNK), F32),
            pltpu.VMEM((2, 4, 2, CHUNK, CHUNK), BF16),
            *[pltpu.VMEM((heads, count, width), F32)] * 3,
            *[pltpu.VMEM((heads * count, width), F32)] * 2,
            pltpu.VMEM((CROSS, heads, *square), BF16),
            pltpu.VMEM((heads, *square), BF16),
            pltpu.VMEM((heads, *square), F32),
            pltpu.VMEM((heads, *square), F32),
            *[pltpu.VMEM(piece, F32)] * 3,
            pltpu.VMEM((CROSS, heads, *square), F32),
            pltpu.VMEM((4, heads, *square), F32),
            pltpu.VMEM((heads, *square), F32),
            *[pltpu.VMEM(piece, F32)] * 3,
            pltpu.VMEM(piece[1:], F32),
            pltpu.SemaphoreType.DMA((5,)),
            pltpu.SemaphoreType.DMA((3,)),
            pltpu.SemaphoreType.DMA((zs - 1,)),
            pltpu.SemaphoreType.DMA((zs - 1,)),
            pltpu.SemaphoreType.DMA((messages,)),
            pltpu.SemaphoreType.DMA((messages,)),
        ],
        compiler_params=pltpu.CompilerParams(
            collective_id=0, has_side_effects=True, vmem_limit_bytes=60 << 20),
        name="exchange",
    )(q, k, v, g, codes)


def on_device(queries, keys, values, out_grad, level_codes):
    count, heads, width = queries.shape
    scale = width ** (-0.5)
    flat = [x.reshape(count * heads, width) for x in (queries, keys, values, out_grad)]
    grads = exchange(scale, lax.axis_size("head"), heads, *flat, level_codes)
    return tuple(x.reshape(count, heads, width) for x in grads)


def solution(mesh):
    return jax.shard_map(
        on_device,
        mesh=mesh,
        in_specs=(
            P("seq", "head", None),
            P("seq", "head", None),
            P("seq", "head", None),
            P("seq", "head", None),
            P(None, ("seq", "head")),
        ),
        out_specs=(P("seq", "head", None), P("seq", "head", None), P("seq", "head", None)),
        check_vma=False,
    )
```

time: 51.8 us -> 42.3 us (0.82)
  Pallas kernels: 50.9 us -> 36.3 us
  local copies, waits for them, and re-layouts: 0 us -> 5.22 us
    pallas_call x1 -> x0, Pallas kernels: 8.88 us -> none  [finish(): pl.pallas_call(finish_kernel, grid=(chunks // steps,), out_shape=(flat, f...]
    pallas_call x1, Pallas kernels: 42.1 us -> 36.3 us  [exchange(): pl.pallas_call(functools.partial(exchange_kernel, scale, zs), out_shape=(...]
    unnamed x0 -> x7, local copies, waits for them, and re-layouts: none -> 5.22 us
where the time goes in v3:
time: 42.3 us; the launch traced here: 42.1 us
  Pallas kernels  36.3 us (86%)
  local copies, waits for them, and re-layouts  5.22 us (12%)
  between operations  0.65 us (2%)
    pallas_call x1, Pallas kernels, exchange(): pl.pallas_call(functools.partial(exchange_kernel, scale, zs), out_shape=(...  36.3 us
    unnamed x7, local copies, waits for them, and re-layouts  5.22 us

profile of v3, /device:TPU:1, one launch (start us, length us, event | category | flops | bytes accessed | tf_op | source)
XLA Modules:
  0.0 42.1 jit_solution(17887378850337846215)
XLA Ops:
  0.6 36.3 %exchange.1 = (bf16[4096,128]{1,0:T(8,128)(2,1)}, bf16[4096,128]{1,0:T(8,128)(2,1)}, bf16[4096,128]{1,0:T(8,128)(2,1)}) custom-call(bf16[4096,128]{1,0:T(8,128)(2,1)} %bitcast.7, bf16[4096,128]{1,0:T(8,128)(2,1)} %bitcast.8, bf16[4096,128]{1,0:T(8,128)(2,1)} %bitcast.9, bf16[4096,128]{1,0:T(8,128)(2,1)} %bitcast.10, s32[21,128]{1,0:T(8,128)} %codes_in.1), custom_call_target="tpu_custom_call" | custom-call | tf_op jit(solution)/shard_map/exchange/pallas_call | solution.py:382
  36.9 0.0 copy-start.1
  36.9 2.6 %copy.11 = bf16[1024,4,128]{2,1,0:T(4,128)(2,1)} copy(bf16[1024,4,128]{2,1,0:T(4,128)(2,1)} %bitcast.13) | data formatting | bytes 2097152
  39.5 0.0 copy-done.1
  39.5 0.0 copy-start
  39.6 1.0 %copy.12 = bf16[1024,4,128]{2,1,0:T(4,128)(2,1)} copy(bf16[1024,4,128]{2,1,0:T(4,128)(2,1)S(1)} %bitcast.12) | data formatting | bytes 2097152
  40.5 0.6 %copy-done = bf16[4096,128]{1,0:T(8,128)(2,1)S(1)} copy-done((bf16[4096,128]{1,0:T(8,128)(2,1)S(1)}, bf16[4096,128]{1,0:T(8,128)(2,1)}, u32[]{:S(2)}) %copy-start) | copy-done | bytes 1048600
  41.2 1.0 %copy.13 = bf16[1024,4,128]{2,1,0:T(4,128)(2,1)} copy(bf16[1024,4,128]{2,1,0:T(4,128)(2,1)S(1)} %bitcast.11) | data formatting | bytes 2097152
Async XLA Ops:
  36.9 2.7 %copy-start.1 = (bf16[4096,128]{1,0:T(8,128)(2,1)S(1)}, bf16[4096,128]{1,0:T(8,128)(2,1)}, u32[]{:S(2)}) copy-start(bf16[4096,128]{1,0:T(8,128)(2,1)} %get-tuple-element.7) | copy-start | bytes 3145732
  39.5 1.6 %copy-start = (bf16[4096,128]{1,0:T(8,128)(2,1)S(1)}, bf16[4096,128]{1,0:T(8,128)(2,1)}, u32[]{:S(2)}) copy-start(bf16[4096,128]{1,0:T(8,128)(2,1)} %get-tuple-element.8) | copy-start | bytes 3145732

commit v4 on v3

--- a/solution.py
+++ b/solution.py
@@ -33,13 +33,6 @@
     return lax.rem(jnp.right_shift(index, bit), 2).astype(F32)
 
 
-def spread(codes, first, count):
-    rows = lax.broadcasted_iota(jnp.int32, (codes.shape[0], count * CHUNK), 0)
-    cols = lax.broadcasted_iota(jnp.int32, (codes.shape[0], count * CHUNK), 1)
-    pick = (rows == first + jnp.right_shift(cols, 7)).astype(F32).astype(BF16)
-    return dot(codes.astype(F32).astype(BF16), pick, TN)
-
-
 def split_heads(flat, tmp, out):
     heads, count, _ = out.shape
     tmp[...] = flat[...].astype(F32)
@@ -69,12 +62,12 @@
 def exchange_kernel(
     scale, zs,
     q_in, k_in, v_in, g_in, codes_in,
-    dq_out, dk_out, dv_out,
-    flat, tmp, qh, kh, vh, gh, gt, lam, codes,
-    one, states, inner, inner_t, mask, weight, dq, dk, dv, flat_k, flat_v, cross, ks,
+    flat_q, flat_k, flat_v,
+    flat, tmp, qh, kh, vh, gh, qt, kt, gt, lam, codes,
+    one, states, inner, inner_t, mask, weight, dq, dk, dv, cross, ks,
     state, r_state, tot, r_tot, r_found,
     level, r_level, r_level0, down, r_down, mid, r_mid,
-    in_sem, out_sem, code_send, code_recv, send, recv,
+    in_sem, code_send, code_recv, send, recv,
 ):
     seq = lax.axis_index("seq")
     z = lax.axis_index("head")
@@ -113,15 +106,14 @@
         c.start()
         return c
 
-    outs = []
-
-    def put(src, dst):
-        c = pltpu.make_async_copy(src, dst, out_sem.at[len(outs)])
-        c.start()
-        outs.append(c)
+    def transpose(src, dst):
+        for h in range(heads):
+            for n in range(chunks):
+                dst[h, :, chunk(n)] = src[h, chunk(n)].T
 
     loads[0].wait()
     split_heads(flat.at[0], tmp, kh)
+    transpose(kh, kt)
     loads[1].wait()
     split_heads(flat.at[1], tmp, vh)
     here.wait()
@@ -131,7 +123,7 @@
         for i in range(2):
             h = 2 * pair + i
             for n in range(chunks):
-                one[i, n] = dot(vh[h, chunk(n)], kh[h, chunk(n)], TN)
+                one[i, n] = dot(kt[h, :, chunk(n)], vh[h, chunk(n)])
             state[h] = total_of(one[i, n] for n in range(chunks))
             for m, (b, (lo, hi), _) in enumerate(PAIRS):
                 acc = total_of(one[i, n] for n in range(lo, hi))
@@ -154,6 +146,7 @@
 
     loads[3].wait()
     split_heads(flat.at[3], tmp, gh)
+    transpose(gh, gt)
 
     s_their.wait_recv()
     up = [[]]
@@ -163,9 +156,7 @@
 
     loads[2].wait()
     split_heads(flat.at[2], tmp, qh)
-    for h in range(heads):
-        for n in range(chunks):
-            gt[h, :, chunk(n)] = gh[h, chunk(n)].T
+    transpose(qh, qt)
 
     def step_up(p):
         up.append([])
@@ -174,16 +165,25 @@
             tot[p, s] = tot[p - 1, s] + r_tot[p - 1, s]
             up[p].append(remote(tot.at[p, s], r_tot.at[p, s], p + 1))
 
-    def spread_codes(first, number):
-        for c in range(chunks):
-            lam[chunk(c), chunk(first, number)] = spread(codes[c], 8 + first, number).astype(BF16)
+    def code_rows():
+        for m in range(INNER + CROSS):
+            for c in range(chunks):
+                line = codes[c, 8 + m : 9 + m, :].astype(F32)
+                lam[m, :, chunk(c)] = jnp.broadcast_to(line, (16, CHUNK)).astype(BF16)
+
+    def by_code(m, matrix, rows):
+        tiles = matrix.reshape(matrix.shape[0] // 16, 16, matrix.shape[1])
+        return (tiles * lam[m, :, rows][None]).reshape(matrix.shape)
+
+    everything = pl.ds(0, count)
 
     def level_grads(bits, h):
-        wide = jnp.concatenate([lam[:, chunk(INNER + b)] * qh[h] for b in bits], axis=1)
-        result = dot(gt[h], wide)
+        query = qt[h]
+        tall = jnp.concatenate([by_code(INNER + b, query, everything) for b in bits], axis=0)
+        result = dot(tall, gh[h])
         for i, b in enumerate(bits):
             level[b, h] = (scale * factor(11 + b) * on_bit(seq, b)) * result[
-                :, i * CHUNK : (i + 1) * CHUNK]
+                i * CHUNK : (i + 1) * CHUNK]
 
     halves = [None] * CROSS
 
@@ -193,27 +193,20 @@
 
     for c in codes_sent:
         c.wait_recv()
-    spread_codes(INNER + 3, 2)
+    code_rows()
     for i in range(2):
-        level_grads((3, 4), theirs + i)
-    send_half(4)
-    send_half(3)
+        level_grads(range(CROSS), theirs + i)
+    for b in (4, 3, 2, 1):
+        send_half(b)
     for i in range(2):
-        level_grads((3, 4), mine + i)
+        level_grads(range(CROSS), mine + i)
+    whole = remote(level.at[0], r_level0, 0)
     step_up(1)
-    spread_codes(0, INNER + 3)
     halves[4].wait_recv()
     now = []
     for s in subs:
         down[0, s] = part(level, s, 4) + part(r_level, s, 3)
         now.append(remote(down.at[0, s], r_down.at[0, s], 4))
-    for i in range(2):
-        level_grads((0, 1, 2), theirs + i)
-    send_half(2)
-    send_half(1)
-    for i in range(2):
-        level_grads((0, 1, 2), mine + i)
-    whole = remote(level.at[0], r_level0, 0)
     step_up(2)
 
     def masks():
@@ -237,8 +230,8 @@
             found = []
             for b, _, (lo, hi) in PAIRS:
                 rows = chunk(lo, hi - lo)
-                wide = lam[rows, chunk(b)] * qh[h, rows]
-                found.append((scale * factor(8 + b)) * dot(gt[h, :, rows], wide))
+                tall = by_code(b, qt[h, :, rows], rows)
+                found.append((scale * factor(8 + b)) * dot(tall, gh[h, rows]))
             for n in range(chunks - 1):
                 acc = total_of(
                     found[m] for m, (_, (lo, hi), _) in enumerate(PAIRS) if lo <= n < hi)
@@ -251,8 +244,8 @@
         for i in range(4):
             rows = chunk(start + i)
             weights = mask[start + i]
-            weight[u % 2, i, 0] = (weights * dot(vh[h, rows], gh[h, rows], NT)).astype(BF16)
-            weight[u % 2, i, 1] = (weights * dot(kh[h, rows], qh[h, rows], NT)).astype(BF16)
+            weight[u % 2, i, 0] = (weights * dot(vh[h, rows], gt[h, :, rows])).astype(BF16)
+            weight[u % 2, i, 1] = (weights * dot(kh[h, rows], qt[h, :, rows])).astype(BF16)
 
     def second_stage(u):
         h, start = u // 2, u % 2 * 4
@@ -264,19 +257,19 @@
             if n < chunks - 1:
                 dk[h, rows] = dot(
                     jnp.concatenate([weight_q, value], axis=1),
-                    jnp.concatenate([query, inner[n, h]], axis=0))
+                    jnp.concatenate([query, inner_t[n, h]], axis=0))
                 dv[h, rows] = dot(
                     jnp.concatenate([weight_v, key], axis=1),
-                    jnp.concatenate([grad, inner_t[n, h]], axis=0))
+                    jnp.concatenate([grad, inner[n, h]], axis=0))
             else:
                 dk[h, rows] = dot(weight_q, query)
                 dv[h, rows] = dot(weight_v, grad)
-            left, right = [weight_q.T], [key]
+            left, right = [kt[h, :, rows]], [weight_q]
             for m, (b, _, (lo, hi)) in enumerate(PAIRS):
                 if lo <= n < hi:
-                    left.append(lam[rows, chunk(b)] * grad)
-                    right.append(states[m, h])
-            dq[h, rows] = dot(jnp.concatenate(left, axis=1), jnp.concatenate(right, axis=0))
+                    left.append(states[m, h])
+                    right.append(by_code(b, gt[h, :, rows], rows))
+            dq[h, :, rows] = dot(jnp.concatenate(left, axis=1), jnp.concatenate(right, axis=0))
 
     def diagonal(u):
         if u > 0:
@@ -285,18 +278,25 @@
             first_stage(u)
 
     def across(h):
-        wide = jnp.concatenate([lam[:, chunk(INNER + b)] * gh[h] for b in range(CROSS)], axis=1)
-        matrix = jnp.concatenate([cross[b, h] for b in range(CROSS)], axis=0)
-        tmp[pl.ds(h, count, stride=heads), :] = dq[h] + dot(wide, matrix)
-
-    def put_queries():
-        flat[0] = tmp[...].astype(BF16)
-        put(flat.at[0], dq_out)
+        matrix = jnp.concatenate([cross[b, h] for b in range(CROSS)], axis=1)
+        for n in range(0, chunks, 2):
+            rows = chunk(n, 2)
+            grad = gt[h, :, rows]
+            tall = jnp.concatenate([by_code(INNER + b, grad, rows) for b in range(CROSS)], axis=0)
+            result = (dq[h, :, rows] + dot(matrix, tall)).astype(BF16)
+            for i in range(2):
+                at = pl.ds((n + i) * CHUNK * heads + h, CHUNK, stride=heads)
+                flat_q[at, :] = result[:, i * CHUNK : (i + 1) * CHUNK].T.astype(F32)
 
     def finish(h):
         at = pl.ds(h, count, stride=heads)
-        flat_k[at, :] = dk[h] + dot(vh[h], ks[h])
-        flat_v[at, :] = dv[h] + dot(kh[h], ks[h], NT)
+        matrix, zero = ks[h], jnp.zeros((CHUNK, CHUNK), BF16)
+        both = jnp.concatenate([
+            jnp.concatenate([matrix.T, zero], axis=1),
+            jnp.concatenate([zero, matrix], axis=1)], axis=0)
+        result = dot(jnp.concatenate([vh[h], kh[h]], axis=1), both)
+        flat_k[at, :] = dk[h] + result[:, :CHUNK]
+        flat_v[at, :] = dv[h] + result[:, CHUNK:]
 
     work = [masks, functools.partial(inner_grads, 0), functools.partial(inner_grads, 2)]
     work += [functools.partial(diagonal, u) for u in range(9)]
@@ -342,7 +342,6 @@
             cross[p + 1, theirs + s // 2, rows] = (value * r_found[p, s]).astype(BF16)
     for h in range(heads):
         across(h)
-    put_queries()
 
     last = []
     whole.wait_recv()
@@ -352,23 +351,17 @@
         last.append(remote(mid.at[3, s], r_mid.at[s], 0))
         rows = pl.ds(s % 2 * half, half)
         ks[mine + s // 2, rows] = (mid[3, s] + part(r_level0, s)).astype(BF16)
-        if s % 2:
-            finish(mine + s // 2)
+    for i in range(2):
+        finish(mine + i)
     for s in subs:
         last[s].wait_recv()
         rows = pl.ds(s % 2 * half, half)
         ks[theirs + s // 2, rows] = (r_mid[s] + r_level0[theirs + s // 2, rows]).astype(BF16)
     for i in range(2):
         finish(theirs + i)
-    flat[1] = flat_k[...].astype(BF16)
-    put(flat.at[1], dk_out)
-    flat[2] = flat_v[...].astype(BF16)
-    put(flat.at[2], dv_out)
 
     for c in sent + codes_sent:
         c.wait_send()
-    for c in outs:
-        c.wait()
 
 
 def exchange(scale, zs, heads, q, k, v, g, codes):
@@ -376,28 +369,29 @@
     chunks = count // CHUNK
     square = (width, width)
     piece = (4, 4, CHUNK // 2, width)
-    any_space = pl.BlockSpec(memory_space=pl.ANY)
+    hbm = pl.BlockSpec(memory_space=pltpu.HBM)
+    vmem = pl.BlockSpec(memory_space=pltpu.VMEM)
     messages = 2 + 16 + 4 + 4 + 1 + 16 + 4
-    flat = jax.ShapeDtypeStruct((heads * count, width), BF16)
+    flat = jax.ShapeDtypeStruct((heads * count, width), F32)
     return pl.pallas_call(
         functools.partial(exchange_kernel, scale, zs),
         out_shape=(flat,) * 3,
-        in_specs=[any_space] * 5,
-        out_specs=(any_space,) * 3,
+        in_specs=[hbm] * 5,
+        out_specs=(vmem,) * 3,
         scratch_shapes=[
             pltpu.VMEM((4, heads * count, width), BF16),
             pltpu.VMEM((heads * count, width), F32),
             *[pltpu.VMEM((heads, count, width), BF16)] * 4,
-            pltpu.VMEM((heads, width, count), BF16),
-            pltpu.VMEM((count, (INNER + CROSS) * width), BF16),
+            *[pltpu.VMEM((heads, width, count), BF16)] * 3,
+            pltpu.VMEM((INNER + CROSS, 16, count), BF16),
             pltpu.VMEM((zs, ROWS, CHUNK), jnp.int32),
             pltpu.VMEM((2, chunks, *square), F32),
             pltpu.VMEM((len(PAIRS), heads, *square), BF16),
             *[pltpu.VMEM((chunks - 1, heads, *square), BF16)] * 2,
             pltpu.VMEM((chunks, CHUNK, CHUNK), F32),
             pltpu.VMEM((2, 4, 2, CHUNK, CHUNK), BF16),
-            *[pltpu.VMEM((heads, count, width), F32)] * 3,
-            *[pltpu.VMEM((heads * count, width), F32)] * 2,
+            pltpu.VMEM((heads, width, count), F32),
+            *[pltpu.VMEM((heads, count, width), F32)] * 2,
             pltpu.VMEM((CROSS, heads, *square), BF16),
             pltpu.VMEM((heads, *square), BF16),
             pltpu.VMEM((heads, *square), F32),
@@ -409,23 +403,53 @@
             *[pltpu.VMEM(piece, F32)] * 3,
             pltpu.VMEM(piece[1:], F32),
             pltpu.SemaphoreType.DMA((5,)),
-            pltpu.SemaphoreType.DMA((3,)),
             pltpu.SemaphoreType.DMA((zs - 1,)),
             pltpu.SemaphoreType.DMA((zs - 1,)),
             pltpu.SemaphoreType.DMA((messages,)),
             pltpu.SemaphoreType.DMA((messages,)),
         ],
         compiler_params=pltpu.CompilerParams(
-            collective_id=0, has_side_effects=True, vmem_limit_bytes=60 << 20),
+            collective_id=0, has_side_effects=True, vmem_limit_bytes=LIMIT),
         name="exchange",
     )(q, k, v, g, codes)
+
+
+LIMIT = 44 << 20
+
+
+def pack_kernel(q_in, k_in, v_in, q_out, k_out, v_out, stage, sem):
+    rows = q_in.shape[0] // 4
+    copies = []
+    for i, (src, dst) in enumerate(((q_in, q_out), (k_in, k_out), (v_in, v_out))):
+        for n in range(4):
+            at = pl.ds(n * rows, rows)
+            stage[i, at] = src[at, :].astype(BF16)
+            c = pltpu.make_async_copy(stage.at[i, at], dst.at[at], sem.at[i, n])
+            c.start()
+            copies.append(c)
+    for c in copies:
+        c.wait()
+
+
+def pack(*flat):
+    shape = flat[0].shape
+    return pl.pallas_call(
+        pack_kernel,
+        out_shape=(jax.ShapeDtypeStruct(shape, BF16),) * 3,
+        in_specs=[pl.BlockSpec(memory_space=pltpu.VMEM)] * 3,
+        out_specs=(pl.BlockSpec(memory_space=pltpu.HBM),) * 3,
+        scratch_shapes=[pltpu.VMEM((3, *shape), BF16), pltpu.SemaphoreType.DMA((3, 4))],
+        compiler_params=pltpu.CompilerParams(vmem_limit_bytes=16 << 20),
+        name="pack",
+    )(*flat)
 
 
 def on_device(queries, keys, values, out_grad, level_codes):
     count, heads, width = queries.shape
     scale = width ** (-0.5)
     flat = [x.reshape(count * heads, width) for x in (queries, keys, values, out_grad)]
-    grads = exchange(scale, lax.axis_size("head"), heads, *flat, level_codes)
+    flat = [pltpu.with_memory_space_constraint(x, pltpu.HBM) for x in flat]
+    grads = pack(*exchange(scale, lax.axis_size("head"), heads, *flat, level_codes))
     return tuple(x.reshape(count, heads, width) for x in grads)
 
 

time: 42.3 us -> 37.9 us (0.90)
  local copies, waits for them, and re-layouts: 5.22 us -> 0.7 us
    unnamed x7 -> x2, local copies, waits for them, and re-layouts: 5.22 us -> 0.7 us
    pallas_call x0 -> x1, Pallas kernels: none -> 1.78 us  [pack(): pl.pallas_call(pack_kernel, out_shape=(jax.ShapeDtypeStruct(shape, BF16),...]
    pallas_call x1, Pallas kernels: 36.3 us -> 34.6 us  [exchange(): pl.pallas_call(functools.partial(exchange_kernel, scale, zs), out_shape=(...]
where the time goes in v4:
time: 37.9 us; the launch traced here: 37.7 us
  Pallas kernels  36.4 us (96%)
  local copies, waits for them, and re-layouts  0.7 us (2%)
  between operations  0.65 us (2%)
    pallas_call x1, Pallas kernels, exchange(): pl.pallas_call(functools.partial(exchange_kernel, scale, zs), out_shape=(...  34.6 us
    pallas_call x1, Pallas kernels, pack(): pl.pallas_call(pack_kernel, out_shape=(jax.ShapeDtypeStruct(shape, BF16),...  1.78 us

profile of v4, /device:TPU:1, one launch (start us, length us, event | category | flops | bytes accessed | tf_op | source)
XLA Modules:
  0.0 37.7 jit_solution(12201768812609955686)
XLA Ops:
  0.6 0.0 copy-start
  0.6 0.7 %copy-done = s32[21,128]{1,0:T(8,128)S(1)} copy-done((s32[21,128]{1,0:T(8,128)S(1)}, s32[21,128]{1,0:T(8,128)}, u32[]{:S(2)}) %copy-start) | copy-done | bytes 10776
  1.3 34.6 %exchange.1 = (f32[4096,128]{1,0:T(8,128)S(1)}, f32[4096,128]{1,0:T(8,128)S(1)}, f32[4096,128]{1,0:T(8,128)S(1)}) custom-call(bf16[4096,128]{1,0:T(8,128)(2,1)} %bitcast.7, bf16[4096,128]{1,0:T(8,128)(2,1)} %bitcast.8, bf16[4096,128]{1,0:T(8,128)(2,1)} %bitcast.9, bf16[4096,128]{1,0:T(8,128)(2,1)} %bitcast.10, s32[21,128]{1,0:T(8,128)S(1)} %copy-done), custom_call_target="tpu_custom_call" | custom-call | tf_op jit(solution)/shard_map/exchange/pallas_call | solution.py:376
  35.9 1.8 %pack.1 = (bf16[4096,128]{1,0:T(8,128)(2,1)}, bf16[4096,128]{1,0:T(8,128)(2,1)}, bf16[4096,128]{1,0:T(8,128)(2,1)}) custom-call(f32[4096,128]{1,0:T(8,128)S(1)} %get-tuple-element.9.q_in, f32[4096,128]{1,0:T(8,128)S(1)} %get-tuple-element.10.k_in, f32[4096,128]{1,0:T(8,128)S(1)} %get-tuple-element.11.v_in), custom_call_target="tpu_custom_call" | custom-call | tf_op jit(solution)/shard_map/pack/pallas_call | solution.py:436
Async XLA Ops:
  0.6 0.7 %copy-start = (s32[21,128]{1,0:T(8,128)S(1)}, s32[21,128]{1,0:T(8,128)}, u32[]{:S(2)}) copy-start(s32[21,128]{1,0:T(8,128)} %codes_in.1) | copy-start | bytes 32260

commit v5 on v4

--- a/solution.py
+++ b/solution.py
@@ -14,6 +14,7 @@
 INNER = 3
 CROSS = 5
 ROWS = 16
+SPLIT = 2
 PARTNERS = (1, 2, 6, 8, 24)
 
 NN = (((1,), (0,)), ((), ()))
@@ -75,10 +76,16 @@
     theirs = 2 - mine
     heads, count, width = qh.shape
     chunks = count // CHUNK
-    subs = range(4)
-    half = CHUNK // 2
+    subs = range(2 * SPLIT)
+    half = CHUNK // SPLIT
     partner = [jnp.bitwise_xor(seq, p) for p in PARTNERS]
 
+    loads = [
+        pltpu.make_async_copy(src, flat.at[i], in_sem.at[i])
+        for i, src in enumerate((k_in, v_in, q_in, g_in))
+    ]
+    here = pltpu.make_async_copy(codes_in.at[pl.ds(0, ROWS)], codes.at[z], in_sem.at[4])
+    loads[0].start()
     barrier = pltpu.get_barrier_semaphore()
     for d in range(1, zs):
         pl.semaphore_signal(
@@ -86,12 +93,7 @@
     for p in partner:
         pl.semaphore_signal(barrier, inc=1, device_id=(p, z), device_id_type=MESH)
 
-    loads = [
-        pltpu.make_async_copy(src, flat.at[i], in_sem.at[i])
-        for i, src in enumerate((k_in, v_in, q_in, g_in))
-    ]
-    here = pltpu.make_async_copy(codes_in.at[pl.ds(0, ROWS)], codes.at[z], in_sem.at[4])
-    for c in loads:
+    for c in loads[1:]:
         c.start()
     here.start()
 
@@ -117,6 +119,16 @@
     loads[1].wait()
     split_heads(flat.at[1], tmp, vh)
     here.wait()
+
+    pl.semaphore_wait(barrier, len(partner) + zs - 1)
+    codes_sent = []
+    for d in range(1, zs):
+        c = pltpu.make_async_remote_copy(
+            src_ref=codes_in.at[pl.ds(0, ROWS)], dst_ref=codes.at[z],
+            send_sem=code_send.at[d - 1], recv_sem=code_recv.at[d - 1],
+            device_id=(seq, lax.rem(z + d, zs)), device_id_type=MESH)
+        c.start()
+        codes_sent.append(c)
 
     @pl.loop(0, heads // 2)
     def _(pair):
@@ -129,20 +141,11 @@
                 acc = total_of(one[i, n] for n in range(lo, hi))
                 states[m, h] = (acc * (scale * factor(8 + b))).astype(BF16)
 
-    pl.semaphore_wait(barrier, len(partner) + zs - 1)
-    codes_sent = []
-    for d in range(1, zs):
-        c = pltpu.make_async_remote_copy(
-            src_ref=codes_in.at[pl.ds(0, ROWS)], dst_ref=codes.at[z],
-            send_sem=code_send.at[d - 1], recv_sem=code_recv.at[d - 1],
-            device_id=(seq, lax.rem(z + d, zs)), device_id_type=MESH)
-        c.start()
-        codes_sent.append(c)
     s_their = remote(state.at[pl.ds(theirs, 2)], r_state.at[pl.ds(theirs, 2)], 0)
     s_mine = remote(state.at[pl.ds(mine, 2)], r_state.at[pl.ds(mine, 2)], 0)
 
     def part(ref, s, *lead):
-        return ref[(*lead, mine + s // 2, pl.ds(s % 2 * half, half))]
+        return ref[(*lead, mine + s // SPLIT, pl.ds(s % SPLIT * half, half))]
 
     loads[3].wait()
     split_heads(flat.at[3], tmp, gh)
@@ -158,12 +161,12 @@
     split_heads(flat.at[2], tmp, qh)
     transpose(qh, qt)
 
-    def step_up(p):
-        up.append([])
-        for s in subs:
-            up[p - 1][s].wait_recv()
-            tot[p, s] = tot[p - 1, s] + r_tot[p - 1, s]
-            up[p].append(remote(tot.at[p, s], r_tot.at[p, s], p + 1))
+    def step_up(p, s):
+        if s == 0:
+            up.append([])
+        up[p - 1][s].wait_recv()
+        tot[p, s] = tot[p - 1, s] + r_tot[p - 1, s]
+        up[p].append(remote(tot.at[p, s], r_tot.at[p, s], p + 1))
 
     def code_rows():
         for m in range(INNER + CROSS):
@@ -175,12 +178,14 @@
         tiles = matrix.reshape(matrix.shape[0] // 16, 16, matrix.shape[1])
         return (tiles * lam[m, :, rows][None]).reshape(matrix.shape)
 
-    everything = pl.ds(0, count)
-
     def level_grads(bits, h):
-        query = qt[h]
-        tall = jnp.concatenate([by_code(INNER + b, query, everything) for b in bits], axis=0)
-        result = dot(tall, gh[h])
+        result = None
+        for n in range(0, chunks, 2):
+            rows = chunk(n, 2)
+            query = qt[h, :, rows]
+            tall = jnp.concatenate([by_code(INNER + b, query, rows) for b in bits], axis=0)
+            found = dot(tall, gh[h, rows])
+            result = found if result is None else result + found
         for i, b in enumerate(bits):
             level[b, h] = (scale * factor(11 + b) * on_bit(seq, b)) * result[
                 i * CHUNK : (i + 1) * CHUNK]
@@ -201,14 +206,13 @@
     for i in range(2):
         level_grads(range(CROSS), mine + i)
     whole = remote(level.at[0], r_level0, 0)
-    step_up(1)
+    for s in subs:
+        step_up(1, s)
     halves[4].wait_recv()
     now = []
     for s in subs:
         down[0, s] = part(level, s, 4) + part(r_level, s, 3)
         now.append(remote(down.at[0, s], r_down.at[0, s], 4))
-    step_up(2)
-
     def masks():
         s_at = lax.broadcasted_iota(jnp.int32, (CHUNK, CHUNK), 0)
         t_at = lax.broadcasted_iota(jnp.int32, (CHUNK, CHUNK), 1)
@@ -306,6 +310,7 @@
             if work:
                 work.pop(0)()
 
+    do(3)
     found = []
     for n, b in enumerate((3, 2, 1)):
         halves[b].wait_recv()
@@ -318,45 +323,50 @@
             mid[n, s] = value
             down[n + 1, s] = value + part(level, s, b) + part(r_level, s, b - 1)
             after.append(remote(down.at[n + 1, s], r_down.at[n + 1, s], b))
-            do()
+            if n < 2:
+                step_up(n + 2, s)
+            else:
+                up[3][s].wait_recv()
+            if SPLIT == 2 or s % 2:
+                do()
         now = after
         if n == 0:
-            step_up(3)
-            for p in range(3):
-                found.append(remote(r_tot.at[p], r_found.at[p], 0))
-        if n == 1:
-            for s in subs:
-                up[3][s].wait_recv()
-            found.append(remote(r_tot.at[3], r_found.at[3], 0))
+            found.append(remote(r_tot.at[0], r_found.at[0], 0))
+        found.append(remote(r_tot.at[n + 1], r_found.at[n + 1], 0))
     do(len(work))
+
+    def cross_states(p):
+        found[p].wait_recv()
+        value = (scale * factor(12 + p)) * on_bit(seq, p + 1)
+        for s in subs:
+            rows = pl.ds(s % SPLIT * half, half)
+            cross[p + 1, mine + s // SPLIT, rows] = (value * r_tot[p, s]).astype(BF16)
+            cross[p + 1, theirs + s // SPLIT, rows] = (value * r_found[p, s]).astype(BF16)
 
     s_mine.wait_recv()
     for h in range(heads):
         cross[0, h] = ((scale * factor(11)) * on_bit(seq, 0) * r_state[h]).astype(BF16)
-    for p in range(4):
-        found[p].wait_recv()
-        value = (scale * factor(12 + p)) * on_bit(seq, p + 1)
-        for s in subs:
-            rows = pl.ds(s % 2 * half, half)
-            cross[p + 1, mine + s // 2, rows] = (value * r_tot[p, s]).astype(BF16)
-            cross[p + 1, theirs + s // 2, rows] = (value * r_found[p, s]).astype(BF16)
-    for h in range(heads):
-        across(h)
-
+    for p in range(3):
+        cross_states(p)
     last = []
     whole.wait_recv()
     for s in subs:
         now[s].wait_recv()
         mid[3, s] = mid[2, s] + r_down[3, s]
         last.append(remote(mid.at[3, s], r_mid.at[s], 0))
-        rows = pl.ds(s % 2 * half, half)
-        ks[mine + s // 2, rows] = (mid[3, s] + part(r_level0, s)).astype(BF16)
+        rows = pl.ds(s % SPLIT * half, half)
+        ks[mine + s // SPLIT, rows] = (mid[3, s] + part(r_level0, s)).astype(BF16)
+        if s == 0:
+            cross_states(3)
+        if s % SPLIT == SPLIT - 1:
+            across(2 * (s // SPLIT))
+            across(2 * (s // SPLIT) + 1)
     for i in range(2):
         finish(mine + i)
     for s in subs:
         last[s].wait_recv()
-        rows = pl.ds(s % 2 * half, half)
-        ks[theirs + s // 2, rows] = (r_mid[s] + r_level0[theirs + s // 2, rows]).astype(BF16)
+        rows = pl.ds(s % SPLIT * half, half)
+        ks[theirs + s // SPLIT, rows] = (r_mid[s] + r_level0[theirs + s // SPLIT, rows]).astype(BF16)
     for i in range(2):
         finish(theirs + i)
 
@@ -368,10 +378,10 @@
     count, width = q.shape[0] // heads, q.shape[1]
     chunks = count // CHUNK
     square = (width, width)
-    piece = (4, 4, CHUNK // 2, width)
+    piece = (4, 2 * SPLIT, CHUNK // SPLIT, width)
     hbm = pl.BlockSpec(memory_space=pltpu.HBM)
     vmem = pl.BlockSpec(memory_space=pltpu.VMEM)
-    messages = 2 + 16 + 4 + 4 + 1 + 16 + 4
+    messages = 2 + 4 + 4 + 1 + 18 * SPLIT
     flat = jax.ShapeDtypeStruct((heads * count, width), F32)
     return pl.pallas_call(
         functools.partial(exchange_kernel, scale, zs),
@@ -448,8 +458,9 @@
     count, heads, width = queries.shape
     scale = width ** (-0.5)
     flat = [x.reshape(count * heads, width) for x in (queries, keys, values, out_grad)]
-    flat = [pltpu.with_memory_space_constraint(x, pltpu.HBM) for x in flat]
-    grads = pack(*exchange(scale, lax.axis_size("head"), heads, *flat, level_codes))
+    *flat, codes = [
+        pltpu.with_memory_space_constraint(x, pltpu.HBM) for x in (*flat, level_codes)]
+    grads = pack(*exchange(scale, lax.axis_size("head"), heads, *flat, codes))
     return tuple(x.reshape(count, heads, width) for x in grads)
 
 

time: 37.9 us -> 37.8 us (level)
  local copies, waits for them, and re-layouts: 0.7 us -> 0 us
  Pallas kernels: 36.4 us -> 37 us
    unnamed x2 -> x0, local copies, waits for them, and re-layouts: 0.7 us -> none
    pallas_call x1, Pallas kernels: 34.6 us -> 35.2 us  [exchange(): pl.pallas_call(functools.partial(exchange_kernel, scale, zs), out_shape=(...]
where the time goes in v5:
time: 37.8 us; the launch traced here: 37.7 us
  Pallas kernels  37 us (98%)
  between operations  0.64 us (2%)
    pallas_call x1, Pallas kernels, exchange(): pl.pallas_call(functools.partial(exchange_kernel, scale, zs), out_shape=(...  35.2 us
    pallas_call x1, Pallas kernels, pack(): pl.pallas_call(pack_kernel, out_shape=(jax.ShapeDtypeStruct(shape, BF16),...  1.78 us

profile of v5, /device:TPU:1, one launch (start us, length us, event | category | flops | bytes accessed | tf_op | source)
XLA Modules:
  0.0 37.7 jit_solution(18118586653924748525)
XLA Ops:
  0.6 35.2 %exchange.1 = (f32[4096,128]{1,0:T(8,128)S(1)}, f32[4096,128]{1,0:T(8,128)S(1)}, f32[4096,128]{1,0:T(8,128)S(1)}) custom-call(bf16[4096,128]{1,0:T(8,128)(2,1)} %bitcast.7, bf16[4096,128]{1,0:T(8,128)(2,1)} %bitcast.8, bf16[4096,128]{1,0:T(8,128)(2,1)} %bitcast.9, bf16[4096,128]{1,0:T(8,128)(2,1)} %bitcast.10, s32[21,128]{1,0:T(8,128)} %codes_in.1), custom_call_target="tpu_custom_call" | custom-call | tf_op jit(solution)/shard_map/exchange/pallas_call | solution.py:386
  35.9 1.8 %pack.1 = (bf16[4096,128]{1,0:T(8,128)(2,1)}, bf16[4096,128]{1,0:T(8,128)(2,1)}, bf16[4096,128]{1,0:T(8,128)(2,1)}) custom-call(f32[4096,128]{1,0:T(8,128)S(1)} %get-tuple-element.9.q_in, f32[4096,128]{1,0:T(8,128)S(1)} %get-tuple-element.10.k_in, f32[4096,128]{1,0:T(8,128)S(1)} %get-tuple-element.11.v_in), custom_call_target="tpu_custom_call" | custom-call | tf_op jit(solution)/shard_map/pack/pallas_call | solution.py:446

commit v6 on v5

--- a/solution.py
+++ b/solution.py
@@ -15,6 +15,7 @@
 CROSS = 5
 ROWS = 16
 SPLIT = 2
+SOONER = 4
 PARTNERS = (1, 2, 6, 8, 24)
 
 NN = (((1,), (0,)), ((), ()))
@@ -39,6 +40,10 @@
     tmp[...] = flat[...].astype(F32)
     for h in range(heads):
         out[h] = tmp[pl.ds(h, count, stride=heads), :].astype(BF16)
+
+
+def far_first(zs):
+    return sorted(range(1, zs), key=lambda d: -min(d, zs - d))
 
 
 def chunk(n, count=1):
@@ -63,7 +68,7 @@
 def exchange_kernel(
     scale, zs,
     q_in, k_in, v_in, g_in, codes_in,
-    flat_q, flat_k, flat_v,
+    out_q, flat_k, flat_v,
     flat, tmp, qh, kh, vh, gh, qt, kt, gt, lam, codes,
     one, states, inner, inner_t, mask, weight, dq, dk, dv, cross, ks,
     state, r_state, tot, r_tot, r_found,
@@ -87,7 +92,7 @@
     here = pltpu.make_async_copy(codes_in.at[pl.ds(0, ROWS)], codes.at[z], in_sem.at[4])
     loads[0].start()
     barrier = pltpu.get_barrier_semaphore()
-    for d in range(1, zs):
+    for d in far_first(zs):
         pl.semaphore_signal(
             barrier, inc=1, device_id=(seq, lax.rem(z + d, zs)), device_id_type=MESH)
     for p in partner:
@@ -96,6 +101,20 @@
     for c in loads[1:]:
         c.start()
     here.start()
+    codes_sent = [
+        pltpu.make_async_remote_copy(
+            src_ref=codes_in.at[pl.ds(0, ROWS)], dst_ref=codes.at[z],
+            send_sem=code_send.at[d - 1], recv_sem=code_recv.at[d - 1],
+            device_id=(seq, lax.rem(z + d, zs)), device_id_type=MESH)
+        for d in far_first(zs)
+    ]
+
+    def enter():
+        pl.semaphore_wait(barrier, len(partner) + zs - 1)
+        for c in codes_sent:
+            c.start()
+
+    pl.when(z >= SOONER)(enter)
 
     sent = []
 
@@ -119,16 +138,6 @@
     loads[1].wait()
     split_heads(flat.at[1], tmp, vh)
     here.wait()
-
-    pl.semaphore_wait(barrier, len(partner) + zs - 1)
-    codes_sent = []
-    for d in range(1, zs):
-        c = pltpu.make_async_remote_copy(
-            src_ref=codes_in.at[pl.ds(0, ROWS)], dst_ref=codes.at[z],
-            send_sem=code_send.at[d - 1], recv_sem=code_recv.at[d - 1],
-            device_id=(seq, lax.rem(z + d, zs)), device_id_type=MESH)
-        c.start()
-        codes_sent.append(c)
 
     @pl.loop(0, heads // 2)
     def _(pair):
@@ -141,25 +150,25 @@
                 acc = total_of(one[i, n] for n in range(lo, hi))
                 states[m, h] = (acc * (scale * factor(8 + b))).astype(BF16)
 
-    s_their = remote(state.at[pl.ds(theirs, 2)], r_state.at[pl.ds(theirs, 2)], 0)
-    s_mine = remote(state.at[pl.ds(mine, 2)], r_state.at[pl.ds(mine, 2)], 0)
-
-    def part(ref, s, *lead):
-        return ref[(*lead, mine + s // SPLIT, pl.ds(s % SPLIT * half, half))]
-
     loads[3].wait()
     split_heads(flat.at[3], tmp, gh)
     transpose(gh, gt)
+
+    loads[2].wait()
+    split_heads(flat.at[2], tmp, qh)
+    transpose(qh, qt)
+
+    pl.when(z < SOONER)(enter)
+    s_their = remote(state.at[pl.ds(theirs, 2)], r_state.at[pl.ds(theirs, 2)], 0)
+    s_mine = remote(state.at[pl.ds(mine, 2)], r_state.at[pl.ds(mine, 2)], 0)
+
+    def part(ref, s, *lead):
+        return ref[(*lead, mine + s // SPLIT, pl.ds(s % SPLIT * half, half))]
 
     s_their.wait_recv()
     up = [[]]
     for s in subs:
         tot[0, s] = part(state, s) + part(r_state, s)
-        up[0].append(remote(tot.at[0, s], r_tot.at[0, s], 1))
-
-    loads[2].wait()
-    split_heads(flat.at[2], tmp, qh)
-    transpose(qh, qt)
 
     def step_up(p, s):
         if s == 0:
@@ -168,8 +177,8 @@
         tot[p, s] = tot[p - 1, s] + r_tot[p - 1, s]
         up[p].append(remote(tot.at[p, s], r_tot.at[p, s], p + 1))
 
-    def code_rows():
-        for m in range(INNER + CROSS):
+    def code_rows(first, number):
+        for m in range(first, first + number):
             for c in range(chunks):
                 line = codes[c, 8 + m : 9 + m, :].astype(F32)
                 lam[m, :, chunk(c)] = jnp.broadcast_to(line, (16, CHUNK)).astype(BF16)
@@ -198,21 +207,27 @@
 
     for c in codes_sent:
         c.wait_recv()
-    code_rows()
+    code_rows(INNER + 4, 1)
     for i in range(2):
-        level_grads(range(CROSS), theirs + i)
-    for b in (4, 3, 2, 1):
+        level_grads((4,), theirs + i)
+    send_half(4)
+    for i in range(2):
+        level_grads((4,), mine + i)
+    code_rows(0, INNER + 4)
+    for i in range(2):
+        level_grads(range(4), theirs + i)
+    for b in (3, 2, 1):
         send_half(b)
-    for i in range(2):
-        level_grads(range(CROSS), mine + i)
-    whole = remote(level.at[0], r_level0, 0)
-    for s in subs:
-        step_up(1, s)
     halves[4].wait_recv()
     now = []
     for s in subs:
         down[0, s] = part(level, s, 4) + part(r_level, s, 3)
         now.append(remote(down.at[0, s], r_down.at[0, s], 4))
+        up[0].append(remote(tot.at[0, s], r_tot.at[0, s], 1))
+    for i in range(2):
+        level_grads(range(4), mine + i)
+    whole = remote(level.at[0], r_level0, 0)
+
     def masks():
         s_at = lax.broadcasted_iota(jnp.int32, (CHUNK, CHUNK), 0)
         t_at = lax.broadcasted_iota(jnp.int32, (CHUNK, CHUNK), 1)
@@ -282,15 +297,21 @@
             first_stage(u)
 
     def across(h):
-        matrix = jnp.concatenate([cross[b, h] for b in range(CROSS)], axis=1)
+        matrix = jnp.concatenate([cross[b, h] for b in range(4)], axis=1)
         for n in range(0, chunks, 2):
             rows = chunk(n, 2)
             grad = gt[h, :, rows]
-            tall = jnp.concatenate([by_code(INNER + b, grad, rows) for b in range(CROSS)], axis=0)
-            result = (dq[h, :, rows] + dot(matrix, tall)).astype(BF16)
+            tall = jnp.concatenate([by_code(INNER + b, grad, rows) for b in range(4)], axis=0)
+            dq[h, :, rows] += dot(matrix, tall)
+
+    def across_last(h):
+        for n in range(0, chunks, 2):
+            rows = chunk(n, 2)
+            extra = dot(cross[4, h], by_code(INNER + 4, gt[h, :, rows], rows))
+            result = (dq[h, :, rows] + extra).astype(BF16)
             for i in range(2):
                 at = pl.ds((n + i) * CHUNK * heads + h, CHUNK, stride=heads)
-                flat_q[at, :] = result[:, i * CHUNK : (i + 1) * CHUNK].T.astype(F32)
+                tmp[at, :] = result[:, i * CHUNK : (i + 1) * CHUNK].T.astype(F32)
 
     def finish(h):
         at = pl.ds(h, count, stride=heads)
@@ -323,31 +344,28 @@
             mid[n, s] = value
             down[n + 1, s] = value + part(level, s, b) + part(r_level, s, b - 1)
             after.append(remote(down.at[n + 1, s], r_down.at[n + 1, s], b))
-            if n < 2:
-                step_up(n + 2, s)
-            else:
-                up[3][s].wait_recv()
+            step_up(n + 1, s)
             if SPLIT == 2 or s % 2:
                 do()
         now = after
-        if n == 0:
-            found.append(remote(r_tot.at[0], r_found.at[0], 0))
-        found.append(remote(r_tot.at[n + 1], r_found.at[n + 1], 0))
+        found.append(remote(r_tot.at[n], r_found.at[n], 0))
     do(len(work))
 
-    def cross_states(p):
-        found[p].wait_recv()
+    def cross_states(p, ref, first):
         value = (scale * factor(12 + p)) * on_bit(seq, p + 1)
         for s in subs:
             rows = pl.ds(s % SPLIT * half, half)
-            cross[p + 1, mine + s // SPLIT, rows] = (value * r_tot[p, s]).astype(BF16)
-            cross[p + 1, theirs + s // SPLIT, rows] = (value * r_found[p, s]).astype(BF16)
+            cross[p + 1, first + s // SPLIT, rows] = (value * ref[p, s]).astype(BF16)
 
     s_mine.wait_recv()
     for h in range(heads):
         cross[0, h] = ((scale * factor(11)) * on_bit(seq, 0) * r_state[h]).astype(BF16)
     for p in range(3):
-        cross_states(p)
+        cross_states(p, r_tot, mine)
+        found[p].wait_recv()
+        cross_states(p, r_found, theirs)
+    for h in range(heads):
+        across(h)
     last = []
     whole.wait_recv()
     for s in subs:
@@ -356,19 +374,22 @@
         last.append(remote(mid.at[3, s], r_mid.at[s], 0))
         rows = pl.ds(s % SPLIT * half, half)
         ks[mine + s // SPLIT, rows] = (mid[3, s] + part(r_level0, s)).astype(BF16)
-        if s == 0:
-            cross_states(3)
-        if s % SPLIT == SPLIT - 1:
-            across(2 * (s // SPLIT))
-            across(2 * (s // SPLIT) + 1)
+        up[3][s].wait_recv()
+    found.append(remote(r_tot.at[3], r_found.at[3], 0))
+    cross_states(3, r_tot, mine)
     for i in range(2):
         finish(mine + i)
+        across_last(mine + i)
     for s in subs:
         last[s].wait_recv()
         rows = pl.ds(s % SPLIT * half, half)
         ks[theirs + s // SPLIT, rows] = (r_mid[s] + r_level0[theirs + s // SPLIT, rows]).astype(BF16)
+    found[3].wait_recv()
+    cross_states(3, r_found, theirs)
     for i in range(2):
         finish(theirs + i)
+        across_last(theirs + i)
+    out_q[...] = tmp[...].astype(BF16)
 
     for c in sent + codes_sent:
         c.wait_send()
@@ -385,7 +406,7 @@
     flat = jax.ShapeDtypeStruct((heads * count, width), F32)
     return pl.pallas_call(
         functools.partial(exchange_kernel, scale, zs),
-        out_shape=(flat,) * 3,
+        out_shape=(jax.ShapeDtypeStruct(flat.shape, BF16), flat, flat),
         in_specs=[hbm] * 5,
         out_specs=(vmem,) * 3,
         scratch_shapes=[
@@ -425,14 +446,16 @@
 
 
 LIMIT = 44 << 20
+PIECES = 4
 
 
 def pack_kernel(q_in, k_in, v_in, q_out, k_out, v_out, stage, sem):
-    rows = q_in.shape[0] // 4
-    copies = []
-    for i, (src, dst) in enumerate(((q_in, q_out), (k_in, k_out), (v_in, v_out))):
-        for n in range(4):
-            at = pl.ds(n * rows, rows)
+    rows = q_in.shape[0] // PIECES
+    copies = [pltpu.make_async_copy(q_in, q_out, sem.at[2, 0])]
+    copies[0].start()
+    for n in range(PIECES):
+        at = pl.ds(n * rows, rows)
+        for i, (src, dst) in enumerate(((k_in, k_out), (v_in, v_out))):
             stage[i, at] = src[at, :].astype(BF16)
             c = pltpu.make_async_copy(stage.at[i, at], dst.at[at], sem.at[i, n])
             c.start()
@@ -448,7 +471,7 @@
         out_shape=(jax.ShapeDtypeStruct(shape, BF16),) * 3,
         in_specs=[pl.BlockSpec(memory_space=pltpu.VMEM)] * 3,
         out_specs=(pl.BlockSpec(memory_space=pltpu.HBM),) * 3,
-        scratch_shapes=[pltpu.VMEM((3, *shape), BF16), pltpu.SemaphoreType.DMA((3, 4))],
+        scratch_shapes=[pltpu.VMEM((2, *shape), BF16), pltpu.SemaphoreType.DMA((3, PIECES))],
         compiler_params=pltpu.CompilerParams(vmem_limit_bytes=16 << 20),
         name="pack",
     )(*flat)

time: 37.8 us -> 37.1 us (0.981)
  Pallas kernels: 37 us -> 36.4 us
    pallas_call x1, Pallas kernels: 35.2 us -> 34.6 us  [exchange(): pl.pallas_call(functools.partial(exchange_kernel, scale, zs), out_shape=(...]
where the time goes in v6:
time: 37.1 us; the launch traced here: 37 us
  Pallas kernels  36.4 us (98%)
  between operations  0.64 us (2%)
    pallas_call x1, Pallas kernels, exchange(): pl.pallas_call(functools.partial(exchange_kernel, scale, zs), out_shape=(...  34.6 us
    pallas_call x1, Pallas kernels, pack(): pl.pallas_call(pack_kernel, out_shape=(jax.ShapeDtypeStruct(shape, BF16),...  1.76 us

profile of v6, /device:TPU:1, one launch (start us, length us, event | category | flops | bytes accessed | tf_op | source)
XLA Modules:
  0.0 37.0 jit_solution(6852111203114695637)
XLA Ops:
  0.6 34.6 %exchange.1 = (bf16[4096,128]{1,0:T(8,128)(2,1)S(1)}, f32[4096,128]{1,0:T(8,128)S(1)}, f32[4096,128]{1,0:T(8,128)S(1)}) custom-call(bf16[4096,128]{1,0:T(8,128)(2,1)} %bitcast.7, bf16[4096,128]{1,0:T(8,128)(2,1)} %bitcast.8, bf16[4096,128]{1,0:T(8,128)(2,1)} %bitcast.9, bf16[4096,128]{1,0:T(8,128)(2,1)} %bitcast.10, s32[21,128]{1,0:T(8,128)} %codes_in.1), custom_call_target="tpu_custom_call" | custom-call | tf_op jit(solution)/shard_map/exchange/pallas_call | solution.py:407
  35.2 1.8 %pack.1 = (bf16[4096,128]{1,0:T(8,128)(2,1)}, bf16[4096,128]{1,0:T(8,128)(2,1)}, bf16[4096,128]{1,0:T(8,128)(2,1)}) custom-call(bf16[4096,128]{1,0:T(8,128)(2,1)S(1)} %get-tuple-element.9.q_in, f32[4096,128]{1,0:T(8,128)S(1)} %get-tuple-element.10.k_in, f32[4096,128]{1,0:T(8,128)S(1)} %get-tuple-element.11.v_in), custom_call_target="tpu_custom_call" | custom-call | tf_op jit(solution)/shard_map/pack/pallas_call | solution.py:469

commit v7 on v6

--- a/solution.py
+++ b/solution.py
@@ -118,13 +118,20 @@
 
     sent = []
 
-    def remote(src, dst, to):
+    top = lax.rem(jnp.right_shift(seq, 4), 2)
+    some = []
+
+    def remote(src, dst, to, sends=None):
         n = len(sent)
         c = pltpu.make_async_remote_copy(
             src_ref=src, dst_ref=dst, send_sem=send.at[n], recv_sem=recv.at[n],
             device_id=(partner[to], z), device_id_type=MESH)
         sent.append(c)
-        c.start()
+        if sends is None:
+            c.start()
+        else:
+            pl.when(sends)(c.start)
+            some.append((n, sends))
         return c
 
     def transpose(src, dst):
@@ -175,7 +182,8 @@
             up.append([])
         up[p - 1][s].wait_recv()
         tot[p, s] = tot[p - 1, s] + r_tot[p - 1, s]
-        up[p].append(remote(tot.at[p, s], r_tot.at[p, s], p + 1))
+        up[p].append(
+            remote(tot.at[p, s], r_tot.at[p, s], p + 1, None if p < 3 else top == 0))
 
     def code_rows(first, number):
         for m in range(first, first + number):
@@ -222,7 +230,7 @@
     now = []
     for s in subs:
         down[0, s] = part(level, s, 4) + part(r_level, s, 3)
-        now.append(remote(down.at[0, s], r_down.at[0, s], 4))
+        now.append(remote(down.at[0, s], r_down.at[0, s], 4, top == 1))
         up[0].append(remote(tot.at[0, s], r_tot.at[0, s], 1))
     for i in range(2):
         level_grads(range(4), mine + i)
@@ -337,10 +345,12 @@
         halves[b].wait_recv()
         after = []
         for s in subs:
-            now[s].wait_recv()
-            value = r_down[n, s]
             if n:
-                value = value + mid[n - 1, s]
+                now[s].wait_recv()
+                value = r_down[n, s] + mid[n - 1, s]
+            else:
+                pl.when(top == 0)(now[s].wait_recv)
+                value = jnp.where(top == 0, r_down[n, s], 0.0)
             mid[n, s] = value
             down[n + 1, s] = value + part(level, s, b) + part(r_level, s, b - 1)
             after.append(remote(down.at[n + 1, s], r_down.at[n + 1, s], b))
@@ -352,10 +362,12 @@
     do(len(work))
 
     def cross_states(p, ref, first):
-        value = (scale * factor(12 + p)) * on_bit(seq, p + 1)
+        value = scale * factor(12 + p)
+        is_on = lax.rem(jnp.right_shift(seq, p + 1), 2) == 1
         for s in subs:
             rows = pl.ds(s % SPLIT * half, half)
-            cross[p + 1, first + s // SPLIT, rows] = (value * ref[p, s]).astype(BF16)
+            cross[p + 1, first + s // SPLIT, rows] = (
+                jnp.where(is_on, value * ref[p, s], 0.0)).astype(BF16)
 
     s_mine.wait_recv()
     for h in range(heads):
@@ -374,8 +386,8 @@
         last.append(remote(mid.at[3, s], r_mid.at[s], 0))
         rows = pl.ds(s % SPLIT * half, half)
         ks[mine + s // SPLIT, rows] = (mid[3, s] + part(r_level0, s)).astype(BF16)
-        up[3][s].wait_recv()
-    found.append(remote(r_tot.at[3], r_found.at[3], 0))
+        pl.when(top == 1)(up[3][s].wait_recv)
+    found.append(remote(r_tot.at[3], r_found.at[3], 0, top == 1))
     cross_states(3, r_tot, mine)
     for i in range(2):
         finish(mine + i)
@@ -384,14 +396,20 @@
         last[s].wait_recv()
         rows = pl.ds(s % SPLIT * half, half)
         ks[theirs + s // SPLIT, rows] = (r_mid[s] + r_level0[theirs + s // SPLIT, rows]).astype(BF16)
-    found[3].wait_recv()
+    pl.when(top == 1)(found[3].wait_recv)
     cross_states(3, r_found, theirs)
     for i in range(2):
         finish(theirs + i)
         across_last(theirs + i)
     out_q[...] = tmp[...].astype(BF16)
 
-    for c in sent + codes_sent:
+    rare = dict(some)
+    for n, c in enumerate(sent):
+        if n in rare:
+            pl.when(rare[n])(c.wait_send)
+        else:
+            c.wait_send()
+    for c in codes_sent:
         c.wait_send()
 
 

time: 37.1 us -> 36.1 us (0.973)
  Pallas kernels: 36.4 us -> 35.4 us
    pallas_call x1, Pallas kernels: 34.6 us -> 33.6 us  [exchange(): pl.pallas_call(functools.partial(exchange_kernel, scale, zs), out_shape=(...]
where the time goes in v7:
time: 36.1 us; the launch traced here: 36 us
  Pallas kernels  35.4 us (98%)
  between operations  0.64 us (2%)
    pallas_call x1, Pallas kernels, exchange(): pl.pallas_call(functools.partial(exchange_kernel, scale, zs), out_shape=(...  33.6 us
    pallas_call x1, Pallas kernels, pack(): pl.pallas_call(pack_kernel, out_shape=(jax.ShapeDtypeStruct(shape, BF16),...  1.76 us

profile of v7, /device:TPU:1, one launch (start us, length us, event | category | flops | bytes accessed | tf_op | source)
XLA Modules:
  0.0 36.0 jit_solution(12339530987551121739)
XLA Ops:
  0.6 33.6 %exchange.1 = (bf16[4096,128]{1,0:T(8,128)(2,1)S(1)}, f32[4096,128]{1,0:T(8,128)S(1)}, f32[4096,128]{1,0:T(8,128)S(1)}) custom-call(bf16[4096,128]{1,0:T(8,128)(2,1)} %bitcast.7, bf16[4096,128]{1,0:T(8,128)(2,1)} %bitcast.8, bf16[4096,128]{1,0:T(8,128)(2,1)} %bitcast.9, bf16[4096,128]{1,0:T(8,128)(2,1)} %bitcast.10, s32[21,128]{1,0:T(8,128)} %codes_in.1), custom_call_target="tpu_custom_call" | custom-call | tf_op jit(solution)/shard_map/exchange/pallas_call | solution.py:425
  34.3 1.8 %pack.1 = (bf16[4096,128]{1,0:T(8,128)(2,1)}, bf16[4096,128]{1,0:T(8,128)(2,1)}, bf16[4096,128]{1,0:T(8,128)(2,1)}) custom-call(bf16[4096,128]{1,0:T(8,128)(2,1)S(1)} %get-tuple-element.9.q_in, f32[4096,128]{1,0:T(8,128)S(1)} %get-tuple-element.10.k_in, f32[4096,128]{1,0:T(8,128)S(1)} %get-tuple-element.11.v_in), custom_call_target="tpu_custom_call" | custom-call | tf_op jit(solution)/shard_map/pack/pallas_call | solution.py:487

commit v8 on v7

--- a/solution.py
+++ b/solution.py
@@ -167,7 +167,7 @@
 
     pl.when(z < SOONER)(enter)
     s_their = remote(state.at[pl.ds(theirs, 2)], r_state.at[pl.ds(theirs, 2)], 0)
-    s_mine = remote(state.at[pl.ds(mine, 2)], r_state.at[pl.ds(mine, 2)], 0)
+    s_mine = remote(state.at[pl.ds(mine, 2)], r_state.at[pl.ds(mine, 2)], 0, mine == 0)
 
     def part(ref, s, *lead):
         return ref[(*lead, mine + s // SPLIT, pl.ds(s % SPLIT * half, half))]
@@ -234,7 +234,7 @@
         up[0].append(remote(tot.at[0, s], r_tot.at[0, s], 1))
     for i in range(2):
         level_grads(range(4), mine + i)
-    whole = remote(level.at[0], r_level0, 0)
+    whole = remote(level.at[0], r_level0, 0, mine != 0)
 
     def masks():
         s_at = lax.broadcasted_iota(jnp.int32, (CHUNK, CHUNK), 0)
@@ -369,9 +369,9 @@
             cross[p + 1, first + s // SPLIT, rows] = (
                 jnp.where(is_on, value * ref[p, s], 0.0)).astype(BF16)
 
-    s_mine.wait_recv()
+    pl.when(mine != 0)(s_mine.wait_recv)
     for h in range(heads):
-        cross[0, h] = ((scale * factor(11)) * on_bit(seq, 0) * r_state[h]).astype(BF16)
+        cross[0, h] = jnp.where(mine != 0, scale * factor(11) * r_state[h], 0.0).astype(BF16)
     for p in range(3):
         cross_states(p, r_tot, mine)
         found[p].wait_recv()
@@ -379,13 +379,14 @@
     for h in range(heads):
         across(h)
     last = []
-    whole.wait_recv()
+    pl.when(mine == 0)(whole.wait_recv)
     for s in subs:
         now[s].wait_recv()
         mid[3, s] = mid[2, s] + r_down[3, s]
         last.append(remote(mid.at[3, s], r_mid.at[s], 0))
         rows = pl.ds(s % SPLIT * half, half)
-        ks[mine + s // SPLIT, rows] = (mid[3, s] + part(r_level0, s)).astype(BF16)
+        ks[mine + s // SPLIT, rows] = (
+            mid[3, s] + jnp.where(mine == 0, part(r_level0, s), 0.0)).astype(BF16)
         pl.when(top == 1)(up[3][s].wait_recv)
     found.append(remote(r_tot.at[3], r_found.at[3], 0, top == 1))
     cross_states(3, r_tot, mine)
@@ -395,7 +396,8 @@
     for s in subs:
         last[s].wait_recv()
         rows = pl.ds(s % SPLIT * half, half)
-        ks[theirs + s // SPLIT, rows] = (r_mid[s] + r_level0[theirs + s // SPLIT, rows]).astype(BF16)
+        ks[theirs + s // SPLIT, rows] = (
+            r_mid[s] + jnp.where(mine == 0, r_level0[theirs + s // SPLIT, rows], 0.0)).astype(BF16)
     pl.when(top == 1)(found[3].wait_recv)
     cross_states(3, r_found, theirs)
     for i in range(2):

time: 36.1 us -> 36.1 us (level)
  no operation moved by 1% of the time
where the time goes in v8:
time: 36.1 us; the launch traced here: 36 us
  Pallas kernels  35.4 us (98%)
  between operations  0.64 us (2%)
    pallas_call x1, Pallas kernels, exchange(): pl.pallas_call(functools.partial(exchange_kernel, scale, zs), out_shape=(...  33.6 us
    pallas_call x1, Pallas kernels, pack(): pl.pallas_call(pack_kernel, out_shape=(jax.ShapeDtypeStruct(shape, BF16),...  1.76 us

profile of v8, /device:TPU:1, one launch (start us, length us, event | category | flops | bytes accessed | tf_op | source)
XLA Modules:
  0.0 36.0 jit_solution(1058419884411334147)
XLA Ops:
  0.6 33.6 %exchange.1 = (bf16[4096,128]{1,0:T(8,128)(2,1)S(1)}, f32[4096,128]{1,0:T(8,128)S(1)}, f32[4096,128]{1,0:T(8,128)S(1)}) custom-call(bf16[4096,128]{1,0:T(8,128)(2,1)} %bitcast.7, bf16[4096,128]{1,0:T(8,128)(2,1)} %bitcast.8, bf16[4096,128]{1,0:T(8,128)(2,1)} %bitcast.9, bf16[4096,128]{1,0:T(8,128)(2,1)} %bitcast.10, s32[21,128]{1,0:T(8,128)} %codes_in.1), custom_call_target="tpu_custom_call" | custom-call | tf_op jit(solution)/shard_map/exchange/pallas_call | solution.py:427
  34.3 1.8 %pack.1 = (bf16[4096,128]{1,0:T(8,128)(2,1)}, bf16[4096,128]{1,0:T(8,128)(2,1)}, bf16[4096,128]{1,0:T(8,128)(2,1)}) custom-call(bf16[4096,128]{1,0:T(8,128)(2,1)S(1)} %get-tuple-element.9.q_in, f32[4096,128]{1,0:T(8,128)S(1)} %get-tuple-element.10.k_in, f32[4096,128]{1,0:T(8,128)S(1)} %get-tuple-element.11.v_in), custom_call_target="tpu_custom_call" | custom-call | tf_op jit(solution)/shard_map/pack/pallas_call | solution.py:489
